TPU v7x, 32 devices: a whole 2x2x4 slice. The times are simulated.
32 devices in a mesh: seq: 2 (over x), fsdp: 16 (over z, y, core).
Axes of the slice: x: 2, y: 2, z: 4, core: 2. Of those that a mesh axis runs over, the one named last changes fastest.
Arguments:
- inputs: bfloat16 [16, 1024, 1536], P('fsdp', 'seq'), may hold values from -6 to 6
- text_states: bfloat16 [16, 64, 1536], P('fsdp'), may hold values from -6 to 6
- adapter_index: int32 [16], P('fsdp'), may hold values from 0 to 7
- norm_gains: float32 [3, 1536], replicated, may hold values from 0.25 to 1.75
- norm_biases: float32 [3, 1536], replicated, may hold values from -1.8 to 1.8
- self_in: bfloat16 [1536, 4608], P('fsdp'), may hold values from -0.15625 to 0.15625
- self_out: bfloat16 [1536, 1536], P('fsdp'), may hold values from -2.5 to 2.5
- cross_query: bfloat16 [1536, 1536], P('fsdp'), may hold values from -0.15625 to 0.15625
- cross_text: bfloat16 [1536, 3072], P('fsdp'), may hold values from -0.15625 to 0.15625
- cross_out: bfloat16 [1536, 1536], P('fsdp'), may hold values from -0.875 to 0.875
- hidden_in: bfloat16 [1536, 6144], P('fsdp'), may hold values from -0.15625 to 0.15625
- hidden_out: bfloat16 [6144, 1536], P('fsdp'), may hold values from -0.078125 to 0.078125
- adapter_down: bfloat16 [8, 16, 19968], P(None, None, 'fsdp'), may hold values from -0.15625 to 0.15625
- adapter_up: bfloat16 [8, 16, 19968], P(None, None, 'fsdp'), may hold values from -0.75 to 0.75
- cotangent: bfloat16 [16, 1024, 1536], P('fsdp', 'seq'), may hold values from -6 to 6
Outputs:
- output: bfloat16 [16, 1024, 1536], P('fsdp', 'seq')
- grad_input: float32 [16, 1024, 1536], P('fsdp', 'seq')
- grad_text: float32 [16, 64, 1536], P('fsdp')
- grad_down: float32 [8, 16, 19968], P(None, None, 'fsdp')
- grad_up: float32 [8, 16, 19968], P(None, None, 'fsdp')
All inputs are finite; a program needn't handle non-finite values.
Results may differ from a plain program's by a relative error of at most 0.022.
Values may be sent and summed in bfloat16 or wider, within the bound.
No kernel may reach another device: no remote copies, remote signals or barrier semaphores. Data moves between devices by JAX's collectives and lax.ppermute only.
A program may use at most 448 MiB of HBM per device.

v0:
```python
from functools import partial

import jax
import jax.numpy as jnp
from jax import lax
from jax.experimental import pallas as pl
from jax.experimental.pallas import tpu as pltpu
from jax.sharding import PartitionSpec as P

HEAD = 64
LANES = 128
QB = 256
BF = jnp.bfloat16
F32 = jnp.float32
SCALE = float(HEAD) ** (-0.5)
SQRT_HALF = 0.7071067811865476
INV_SQRT_2PI = 0.3989422804014327
MIB = 1024 * 1024
VMEM_LIMIT = 60 * MIB
COST = 1.0
FEED_BLOCK = 512


def mm(a, b):
    return lax.dot_general(a, b, (((1,), (0,)), ((), ())), preferred_element_type=F32)


def mm_nt(a, b):
    return lax.dot_general(a, b, (((1,), (1,)), ((), ())), preferred_element_type=F32)


def mm_tn(a, b):
    return lax.dot_general(a, b, (((0,), (0,)), ((), ())), preferred_element_type=F32)


def norm_stats(values):
    centered = values - jnp.mean(values, -1, keepdims=True)
    variance = jnp.mean(centered * centered, -1, keepdims=True)
    inverse = lax.rsqrt(variance + 1e-05)
    return centered * inverse, inverse


def layer_norm(values, gains, biases):
    unit, _ = norm_stats(values)
    return unit * gains + biases


def norm_back(values, gains, gradient):
    unit, inverse = norm_stats(values)
    scaled = gradient * gains
    mean_one = jnp.mean(scaled, -1, keepdims=True)
    mean_two = jnp.mean(scaled * unit, -1, keepdims=True)
    return inverse * (scaled - mean_one - unit * mean_two)


def whole(shape):
    return pl.BlockSpec(shape, lambda *_: (0,) * len(shape))


def once(shape):
    return pl.BlockSpec(shape, lambda *_: (0,) * len(shape), pipeline_mode=pl.Buffered(1))


def params(count=1, limit=None):
    return pltpu.CompilerParams(
        dimension_semantics=("arbitrary",) * count if count else None, vmem_limit_bytes=limit or VMEM_LIMIT
    )


def cost(flops, moved, special=0):
    return pl.CostEstimate(
        flops=int(flops * COST), bytes_accessed=int(moved * COST), transcendentals=int(special * COST)
    )


def window(packed, start, width, rows=None, steps=1, step=0):
    block = width // steps
    rows = packed.shape[0] if rows is None else rows
    if start % block == 0 and block % LANES == 0:
        base = start // block
        return packed, pl.BlockSpec((rows, block), lambda *at: (0, base + (at[step] if steps > 1 else 0)))
    return packed[:, start : start + width], pl.BlockSpec(
        (rows, block), lambda *at: (0, at[step] if steps > 1 else 0)
    )


def norm_kernel(place_ref, *refs):
    count = len(refs) - 5
    parts, (gain_ref, bias_ref, down_ref, normed_ref, lat_ref) = refs[:count], refs[count:]
    step = 128
    for index, part_ref in enumerate(parts):
        base = place_ref[index] * part_ref.shape[0]

        def some(at, carry):
            rows = pl.ds(pl.multiple_of(at * step, step), step)
            into = pl.ds(pl.multiple_of(base + at * step, step), step)
            normed = layer_norm(part_ref[rows, :].astype(F32), gain_ref[...], bias_ref[...]).astype(BF)
            normed_ref[into, :] = normed
            lat_ref[into, :] = mm_nt(normed, down_ref[...]).astype(BF)
            return carry

        lax.fori_loop(0, part_ref.shape[0] // step, some, 0)


def smem():
    return pl.BlockSpec(memory_space=pltpu.SMEM)


def norm_project(places, parts, gains, biases, down):
    model = parts[0].shape[1]
    frames = sum(part.shape[0] for part in parts)
    ranks = down.shape[0]
    return pl.pallas_call(
        norm_kernel,
        in_specs=[smem()] + [whole(item.shape) for item in parts + [gains, biases, down]],
        out_specs=[whole((frames, model)), whole((frames, ranks))],
        out_shape=[jax.ShapeDtypeStruct((frames, model), BF), jax.ShapeDtypeStruct((frames, ranks), BF)],
        grid=(1,),
        compiler_params=params(1),
        cost_estimate=cost(2 * frames * model * ranks, 4 * frames * model),
        name="norm_project",
    )(places, *parts, gains, biases, down)


def qkv_kernel(normed_ref, lat_ref, up_ref, w_ref, out_ref):
    step = 256

    def some(at, carry):
        rows = pl.ds(pl.multiple_of(at * step, step), step)
        out_ref[rows, :] = (mm(normed_ref[rows, :], w_ref[...]) + mm(lat_ref[rows, :], up_ref[...])).astype(BF)
        return carry

    lax.fori_loop(0, normed_ref.shape[0] // step, some, 0)


def qkv_project(normed, latent, up, packed, start, width):
    row_count, model = normed.shape
    ranks = latent.shape[1]
    steps = 3 if (width // 3) % LANES == 0 else 1
    operand, spec = window(packed, start, width, steps=steps)
    block = width // steps
    if steps == 3:
        up_spec = pl.BlockSpec((None, ranks, block), lambda at: (at, 0, 0))
    else:
        up = up.transpose(1, 0, 2).reshape(ranks, width)
        up_spec = whole(up.shape)
    return pl.pallas_call(
        qkv_kernel,
        grid=(steps,),
        in_specs=[whole(normed.shape), whole(latent.shape), up_spec, spec],
        out_specs=pl.BlockSpec((row_count, block), lambda at: (0, at)),
        out_shape=jax.ShapeDtypeStruct((row_count, width), BF),
        compiler_params=params(1, 42 * MIB),
        cost_estimate=cost(2 * row_count * model * width, 2 * (row_count + width) * model),
        name="qkv_project",
    )(normed, latent, up, operand)


def tri_start(at):
    return QB * at * (at + 1) // 2


def attend_kernel(place_ref, q_ref, k_ref, v_ref, out_ref, prob_ref, *refs):
    sent, (val_t_ref, out_t_ref) = refs[:-2], refs[-2:]
    frames = q_ref.shape[0]
    lane = lax.broadcasted_iota(jnp.int32, (1, LANES), 1) // HEAD
    val_t_ref[...] = v_ref[...].T
    square = (QB, QB)
    keep_tri = lax.broadcasted_iota(jnp.int32, square, 0) <= lax.broadcasted_iota(jnp.int32, square, 1)

    def scores(half, at):
        stop = (at + 1) * QB
        query = q_ref[at * QB : stop, :] * jnp.where(lane == half, SCALE, 0.0).astype(BF)
        last = jnp.where(keep_tri, mm_nt(k_ref[stop - QB : stop, :], query), -1e30)
        if at == 0:
            return last
        return jnp.concatenate([mm_nt(k_ref[0 : stop - QB, :], query), last], 0)

    turns = [(half, at) for at in range(frames // QB) for half in range(2)]
    score = scores(*turns[0])
    for index, (half, at) in enumerate(turns):
        stop = (at + 1) * QB
        own = slice(half * HEAD, (half + 1) * HEAD)
        later = scores(*turns[index + 1]) if index + 1 < len(turns) else None
        raised = jnp.exp(score - jnp.max(score, 0, keepdims=True))
        prob = (raised * (1.0 / jnp.sum(raised, 0, keepdims=True))).astype(BF)
        prob_ref[half, tri_start(at) : tri_start(at) + stop, :] = prob
        out_t_ref[own, at * QB : stop] = mm(val_t_ref[own, 0:stop], prob)
        score = later
    out_ref[...] = out_t_ref[...].T.astype(BF)
    for index, sent_ref in enumerate(sent):
        size = sent_ref.shape[0]
        at = place_ref[1] * len(sent) + index
        sent_ref[...] = out_ref[pl.ds(pl.multiple_of(at * size, size), size), :]


def pair_specs(frames, width):
    pairs = width // LANES
    return [pl.BlockSpec((frames, LANES), lambda at, part=part: (0, part * pairs + at)) for part in range(3)]


def attend(places, sizes, triple, width):
    frames = triple.shape[0]
    pairs = width // LANES
    tri = tri_start(frames // QB)
    return pl.pallas_call(
        attend_kernel,
        grid=(pairs,),
        in_specs=[smem()] + pair_specs(frames, width),
        out_specs=[
            pl.BlockSpec((frames, LANES), lambda at: (0, at)),
            pl.BlockSpec((2, tri, QB), lambda at: (at, 0, 0)),
        ]
        + [pl.BlockSpec((size, LANES), lambda at: (0, at)) for size in sizes],
        out_shape=[
            jax.ShapeDtypeStruct((frames, width), BF),
            jax.ShapeDtypeStruct((2 * pairs, tri, QB), BF),
        ]
        + [jax.ShapeDtypeStruct((size, width), BF) for size in sizes],
        scratch_shapes=[pltpu.VMEM((LANES, frames), BF), pltpu.VMEM((LANES, frames), F32)],
        compiler_params=params(1),
        cost_estimate=cost(
            8 * tri * QB * HEAD * pairs, 2 * (4 * frames * width + 2 * pairs * tri * QB), 2 * pairs * tri * QB
        ),
        name="attend",
    )(places, triple, triple, triple)


def attend_back_kernel(place_ref, q_ref, k_ref, v_ref, out_ref, prob_ref, *refs):
    pieces, (back_ref, grad_ref, key_t_ref, dq_t_ref, dk_acc, dv_acc) = refs[:-6], refs[-6:]
    frames = q_ref.shape[0]
    for index, piece_ref in enumerate(pieces):
        size = piece_ref.shape[0]
        count = max(len(pieces) // 2, 1)
        at = place_ref[index // count] * count + index % count if len(pieces) > 1 else 0
        grad_ref[pl.ds(pl.multiple_of(at * size, size), size), :] = piece_ref[...]
    lane = lax.broadcasted_iota(jnp.int32, (1, LANES), 1) // HEAD
    key_t_ref[...] = k_ref[...].T
    dk_acc[...] = jnp.zeros_like(dk_acc)
    dv_acc[...] = jnp.zeros_like(dv_acc)
    turns = [(half, at) for at in range(frames // QB) for half in range(2)]

    def start(half, at):
        rows = slice(at * QB, (at + 1) * QB)
        grad = grad_ref[rows, :] * jnp.where(lane == half, 1.0, 0.0).astype(BF)
        return grad, mm_nt(v_ref[0 : (at + 1) * QB, :], grad)

    ready = start(*turns[0])
    for index, (half, at) in enumerate(turns):
        stop = (at + 1) * QB
        rows = slice(at * QB, stop)
        own = slice(half * HEAD, (half + 1) * HEAD)
        grad, prob_grad = ready
        if half == 0:
            product = (out_ref[rows, :].astype(F32) * grad_ref[rows, :].astype(F32)).T
        if index + 1 < len(turns):
            ready = start(*turns[index + 1])
        query = q_ref[rows, :] * jnp.where(lane == half, SCALE, 0.0).astype(BF)
        delta = jnp.sum(product[own, :], 0, keepdims=True)
        prob = prob_ref[half, tri_start(at) : tri_start(at) + stop, :]
        dv_acc[0:stop, :] += mm(prob, grad)
        score_grad = (prob.astype(F32) * (prob_grad - delta)).astype(BF)
        dk_acc[0:stop, :] += mm(score_grad, query)
        dq_t_ref[own, rows] = mm(key_t_ref[own, 0:stop], score_grad)
    back_ref[0] = (dq_t_ref[...].T * SCALE).astype(BF)
    back_ref[1] = dk_acc[...].astype(BF)
    back_ref[2] = dv_acc[...].astype(BF)


def attend_back(places, triple, attended, pieces, probs, width):
    frames = triple.shape[0]
    pairs = width // LANES
    tri = tri_start(frames // QB)
    column = pl.BlockSpec((frames, LANES), lambda at: (0, at))
    return pl.pallas_call(
        attend_back_kernel,
        grid=(pairs,),
        in_specs=[smem()]
        + pair_specs(frames, width)
        + [column, pl.BlockSpec((2, tri, QB), lambda at: (at, 0, 0))]
        + [pl.BlockSpec((piece.shape[0], LANES), lambda at: (0, at)) for piece in pieces],
        out_specs=pl.BlockSpec((3, frames, LANES), lambda at: (0, 0, at)),
        out_shape=jax.ShapeDtypeStruct((3, frames, width), BF),
        scratch_shapes=[
            pltpu.VMEM((frames, LANES), BF),
            pltpu.VMEM((LANES, frames), BF),
            pltpu.VMEM((LANES, frames), F32),
            pltpu.VMEM((frames, LANES), F32),
            pltpu.VMEM((frames, LANES), F32),
        ],
        compiler_params=params(1, 42 * MIB),
        cost_estimate=cost(16 * tri * QB * HEAD * pairs, 2 * (8 * frames * width + 2 * pairs * tri * QB)),
        name="attend_back",
    )(places, triple, triple, triple, attended, probs, *pieces)


def feed_kernel(count, based, *refs):
    pieces, refs = refs[:count], refs[count:]
    bases, refs = refs[:based], refs[based:]
    cot_ref, down_in_ref, up_in_ref, down_out_ref, up_out_ref, w_in_ref, w_out_ref = refs[:7]
    out_refs, gu_refs, refs = refs[7 : 7 + count], refs[7 + count : 7 + 2 * count], refs[7 + 2 * count :]
    (
        gdown_in_ref, gup_in_ref, gdown_out_ref, gup_out_ref, normed_ref,
        out_acc, gu_acc, lat_in, glat_out, lat_acc, glat_acc, lat_t, glat_t,
    ) = refs
    at = pl.program_id(0)

    @pl.when(at == 0)
    def _():
        start = 0
        for piece_ref in pieces:
            normed_ref[start : start + piece_ref.shape[0], :] = piece_ref[...]
            start += piece_ref.shape[0]
        latent = mm_nt(normed_ref[...], down_in_ref[...]).astype(BF)
        glat = mm_nt(cot_ref[...], up_out_ref[...]).astype(BF)
        lat_in[...] = latent
        glat_out[...] = glat
        lat_t[...] = latent.astype(F32).T.astype(BF)
        glat_t[...] = glat.astype(F32).T.astype(BF)
        start = 0
        for base_ref in bases:
            out_acc[start : start + base_ref.shape[0], :] = base_ref[...]
            start += base_ref.shape[0]
        if not bases:
            out_acc[...] = jnp.zeros_like(out_acc)
        gu_acc[...] = jnp.zeros_like(gu_acc)
        lat_acc[...] = jnp.zeros_like(lat_acc)
        glat_acc[...] = jnp.zeros_like(glat_acc)

    w_in = w_in_ref[...]
    w_out = w_out_ref[...]
    pre = mm(normed_ref[...], w_in) + mm(lat_in[...], up_in_ref[...])
    act_grad = mm_nt(cot_ref[...], w_out) + mm(glat_out[...], down_out_ref[...])
    cdf = 0.5 * (1.0 + lax.erf(pre * SQRT_HALF))
    slope = cdf + pre * (jnp.exp(-0.5 * pre * pre) * INV_SQRT_2PI)
    act = (pre * cdf).astype(BF)
    pre_grad = (act_grad * slope).astype(BF)
    out_acc[...] += mm(act, w_out)
    gu_acc[...] += mm_nt(pre_grad, w_in)
    lat_acc[...] += mm_nt(act, down_out_ref[...])
    glat_acc[...] += mm_nt(pre_grad, up_in_ref[...])
    gup_in_ref[...] = mm(lat_t[...], pre_grad)
    gdown_out_ref[...] = mm(glat_t[...], act)

    @pl.when(at == pl.num_programs(0) - 1)
    def _():
        latent = lat_acc[...].astype(BF)
        glat = glat_acc[...].astype(BF)
        start = 0
        for out_ref, gu_ref in zip(out_refs, gu_refs):
            rows = slice(start, start + out_ref.shape[0])
            out_ref[...] = (out_acc[rows, :] + mm(latent[rows], up_out_ref[...])).astype(out_ref.dtype)
            gu_ref[...] = (gu_acc[rows, :] + mm(glat[rows], down_in_ref[...])).astype(gu_ref.dtype)
            start += out_ref.shape[0]
        gup_out_ref[...] = mm(latent.astype(F32).T.astype(BF), cot_ref[...])
        gdown_in_ref[...] = mm(glat.astype(F32).T.astype(BF), normed_ref[...])


def feed_forward(pieces, bases, cotangent, block_at, down_in, up_in, down_out, up_out, weights, hidden, kind):
    model = cotangent.shape[1]
    row_count = sum(item.shape[0] for item in pieces)
    rank = down_in.shape[0]
    block = FEED_BLOCK if hidden % FEED_BLOCK == 0 else hidden
    w_in, in_spec, w_out, out_spec = weights(block)
    main = pl.BlockSpec((row_count, model), lambda at: (block_at, 0))
    slim = pl.BlockSpec((rank, block), lambda at: (0, at))
    small = whole((rank, model))
    return pl.pallas_call(
        partial(feed_kernel, len(pieces), len(bases)),
        grid=(hidden // block,),
        in_specs=[once(item.shape) for item in pieces + bases]
        + [main, small, slim, slim, small, in_spec, out_spec],
        out_specs=[whole(item.shape) for item in pieces] * 2 + [small, slim, slim, small],
        out_shape=[jax.ShapeDtypeStruct(item.shape, kind) for item in pieces]
        + [jax.ShapeDtypeStruct(item.shape, BF) for item in pieces]
        + [
            jax.ShapeDtypeStruct((rank, model), F32),
            jax.ShapeDtypeStruct((rank, hidden), F32),
            jax.ShapeDtypeStruct((rank, hidden), F32),
            jax.ShapeDtypeStruct((rank, model), F32),
        ],
        scratch_shapes=[pltpu.VMEM((row_count, model), BF)]
        + [pltpu.VMEM((row_count, model), F32)] * 2
        + [pltpu.VMEM((row_count, rank), BF)] * 2
        + [pltpu.VMEM((row_count, rank), F32)] * 2
        + [pltpu.VMEM((rank, row_count), BF)] * 2,
        compiler_params=params(1),
        cost_estimate=cost(8 * row_count * model * hidden, 4 * hidden * model, 2 * row_count * hidden),
        name="feed_forward",
    )(*pieces, *bases, cotangent, down_in, up_in, down_out, up_out, w_in, w_out)


def spread_heads(rows_ref, into_ref, model):
    keys = rows_ref.shape[0]
    wide = 4 * HEAD
    row = lax.broadcasted_iota(jnp.int32, (4 * keys, wide), 0) // keys
    col = lax.broadcasted_iota(jnp.int32, (4 * keys, wide), 1) // HEAD
    mask = jnp.where(row == col, 1.0, 0.0).astype(BF)

    def some(group, carry):
        part = rows_ref[:, pl.ds(pl.multiple_of(group * wide, wide), wide)]
        into = pl.ds(pl.multiple_of(group * 4 * keys, 4 * keys), 4 * keys)
        into_ref[into, :] = jnp.concatenate([part] * 4, 0) * mask
        return carry

    lax.fori_loop(0, model // wide, some, 0)


def head_total(values, keys, reduce):
    split = values.reshape(4, keys, values.shape[1])
    return jnp.broadcast_to(reduce(split, 1, keepdims=True), split.shape).reshape(values.shape)


def each(count, step, work):
    def some(at, carry):
        work(pl.ds(pl.multiple_of(at * step, step), step))
        return carry

    lax.fori_loop(0, count // step, some, 0)


def weight_copies(plan, place_ref, sources, hold_ref, sem_ref):
    model = hold_ref.shape[1]
    groups = []
    for index, (start, extra) in enumerate(plan):
        if extra is None:
            pairs = [(sources[0].at[:, pl.ds(start, model)], hold_ref.at[index])]
        else:
            half = model // 2
            here, there = [pl.ds(pl.multiple_of(place_ref[at] * half, half), half) for at in range(2)]
            pairs = [(sources[0].at[:, pl.ds(start, half)], hold_ref.at[index, :, here])]
            for at in range(2):
                rows = pl.ds(pl.multiple_of(place_ref[2 + at] * half, half), half)
                pairs.append((sources[extra + at], hold_ref.at[index, rows, there]))
        groups.append(
            [pltpu.make_async_copy(src, dst, sem_ref.at[index, at]) for at, (src, dst) in enumerate(pairs)]
        )
    return groups


def source_count(plan):
    return 1 + 2 * sum(extra is not None for _, extra in plan)


def start_all(copies):
    for copy in copies:
        copy.start()


def wait_all(copies):
    for copy in copies:
        copy.wait()


def middle_kernel(plan, place_ref, *refs):
    sources, refs = refs[: source_count(plan)], refs[source_count(plan) :]
    inputs_ref, adapt_ref, gain_ref, bias_ref, keys_ref, values_ref = refs[:6]
    pieces = refs[6:-13]
    (
        attended_ref, resid1_ref, normed2_ref, query_ref, probs_ref, crossed_ref, resid2_ref, normed3_ref, lat_ref,
        hold_ref, key_wide, value_wide, sem_ref,
    ) = refs[-13:]
    model = inputs_ref.shape[1]
    keys = keys_ref.shape[0]
    rows = inputs_ref.shape[0]
    wide = 4 * HEAD
    copies = weight_copies(plan, place_ref, sources, hold_ref, sem_ref)
    start_all(copies[0])
    for index, piece_ref in enumerate(pieces):
        size = piece_ref.shape[1]
        attended_ref[:, pl.ds(pl.multiple_of(place_ref[index] * size, size), size)] = piece_ref[...]
    spread_heads(keys_ref, key_wide, model)
    spread_heads(values_ref, value_wide, model)

    def adapted(moving_ref, index, store):
        latent = mm_nt(moving_ref[...], adapt_ref[32 * index : 32 * index + 16, :]).astype(BF)
        lat_ref[:, 16 * index : 16 * index + 16] = latent
        wait_all(copies[index])
        if index < 2:
            start_all(copies[index + 1])

        def some(cols):
            store(
                cols,
                mm(moving_ref[...], hold_ref[index, :, cols])
                + mm(latent, adapt_ref[32 * index + 16 : 32 * index + 32, cols]),
            )

        each(model, 512, some)

    def add_first(cols, value):
        resid1_ref[:, cols] = inputs_ref[:, cols].astype(F32) + value

    def add_second(cols, value):
        resid2_ref[:, cols] = resid1_ref[:, cols] + value

    def keep_query(cols, value):
        query_ref[:, cols] = value.astype(BF)

    def normed(values_at, into_ref, which):
        def some(part):
            into_ref[part, :] = layer_norm(
                values_at[part, :], gain_ref[which : which + 1, :], bias_ref[which : which + 1, :]
            ).astype(BF)

        each(rows, 64, some)

    def cross(lanes):
        score = mm_nt(key_wide[lanes, :], query_ref[:, lanes]) * SCALE
        raised = jnp.exp(score - head_total(score, keys, jnp.max))
        prob = (raised / head_total(raised, keys, jnp.sum)).astype(BF)
        probs_ref[lanes, :] = prob
        crossed_ref[:, lanes] = mm_tn(prob, value_wide[lanes, :]).astype(BF)

    adapted(attended_ref, 0, add_first)
    normed(resid1_ref, normed2_ref, 1)
    adapted(normed2_ref, 1, keep_query)
    each(model, wide, cross)
    adapted(crossed_ref, 2, add_second)
    normed(resid2_ref, normed3_ref, 2)


def middle(places, own, own_spec, others, inputs, at, blocks, sources, plan, adapters, gains, biases, keys, values):
    rows, model = own_spec[0], inputs.shape[1]
    spread = model // HEAD * keys.shape[0]
    shape = lambda kind, dims=(rows, model): jax.ShapeDtypeStruct(dims, kind)
    flat = lambda dims: pl.BlockSpec(dims, lambda _, ref: (0,) * len(dims))
    shapes = [shape(kind) for kind in (BF, F32, BF, BF)]
    shapes += [shape(BF, (spread, rows)), shape(BF), shape(F32), shape(BF), shape(BF, (rows, 48))]
    return pl.pallas_call(
        partial(middle_kernel, plan),
        grid_spec=pltpu.PrefetchScalarGridSpec(
            num_scalar_prefetch=1,
            grid=(1,),
            in_specs=[pl.BlockSpec(memory_space=pl.ANY)] * len(sources)
            + [pl.BlockSpec((rows, model), lambda _, ref: (at, 0))]
            + [flat(item.shape) for item in (adapters, gains, biases, keys, values)]
            + [pl.BlockSpec(own_spec, lambda _, ref: (ref[0] * blocks + at, 0) if others else (at, 0))]
            + [flat(item.shape) for item in others],
            out_specs=[flat(item.shape) for item in shapes],
            scratch_shapes=[
                pltpu.VMEM((3, model, model), BF),
                pltpu.VMEM((spread, 4 * HEAD), BF),
                pltpu.VMEM((spread, 4 * HEAD), BF),
                pltpu.SemaphoreType.DMA((3, 3)),
            ],
        ),
        out_shape=shapes,
        compiler_params=params(),
        cost_estimate=cost(6 * rows * model * model, 6 * model * model + 24 * rows * model),
        name="middle",
    )(places, *sources, inputs, adapters, gains, biases, keys, values, own, *others)


def middle_back_kernel(plan, split, place_ref, *refs):
    sources, refs = refs[: source_count(plan)], refs[source_count(plan) :]
    (
        cot_ref, gu_ref, more_ref, attended_ref, resid1_ref, normed2_ref, query_ref, probs_ref, crossed_ref, resid2_ref,
        lat_ref, adapt_ref, gain_ref, keys_ref, values_ref,
    ) = refs[:15]
    refs = refs[15:]
    outs = refs[: 2 if split else 1]
    resid1_grad_ref, memory_ref, small_ref, hold_ref, key_wide, value_wide, work_ref, low_ref, sem_ref = refs[len(outs) :]
    rows, model = cot_ref.shape
    keys = keys_ref.shape[0]
    wide = 4 * HEAD
    copies = weight_copies(plan, place_ref, sources, hold_ref, sem_ref)
    start_all(copies[2])
    spread_heads(keys_ref, key_wide, model)
    spread_heads(values_ref, value_wide, model)

    def first(part):
        gradient = gu_ref[part, :].astype(F32) + more_ref[part, :].astype(F32)
        value = cot_ref[part, :].astype(F32) + norm_back(resid2_ref[part, :], gain_ref[2:3, :], gradient)
        resid1_grad_ref[part, :] = value
        low_ref[part, :] = value.astype(BF)

    def second(part):
        value = resid1_grad_ref[part, :] + norm_back(resid1_ref[part, :], gain_ref[1:2, :], work_ref[part, :])
        resid1_grad_ref[part, :] = value
        low_ref[part, :] = value.astype(BF)

    def back(moving_ref, index, store):
        down = slice(32 * index, 32 * index + 16)
        upper = slice(32 * index + 16, 32 * index + 32)
        glat = mm_nt(low_ref[...], adapt_ref[upper, :]).astype(BF)
        glat_t = glat.astype(F32).T.astype(BF)
        lat_t = lat_ref[:, 16 * index : 16 * index + 16].astype(F32).T.astype(BF)
        wait_all(copies[index])
        if index:
            start_all(copies[index - 1])

        def some(cols):
            small_ref[down, cols] = mm(glat_t, moving_ref[:, cols])
            small_ref[upper, cols] = mm(lat_t, low_ref[:, cols])
            store(cols, mm_nt(low_ref[...], hold_ref[index, cols, :]) + mm(glat, adapt_ref[down, cols]))

        each(model, 512, some)

    def keep(cols, value):
        work_ref[:, cols] = value

    def cross(lanes):
        part = work_ref[:, lanes].astype(BF)
        prob = probs_ref[lanes, :]
        wide_prob = prob.astype(F32)
        weighted = wide_prob * mm_nt(value_wide[lanes, :], part)
        score_grad = (weighted - wide_prob * head_total(weighted, keys, jnp.sum)).astype(BF)
        low_ref[:, lanes] = (mm_tn(score_grad, key_wide[lanes, :]) * SCALE).astype(BF)
        key_full = mm(score_grad, query_ref[:, lanes])
        value_full = mm(prob, part)
        col = lax.broadcasted_iota(jnp.int32, (keys, wide), 1) // HEAD
        key_sum, value_sum = key_full[:keys], value_full[:keys]
        for head in range(1, 4):
            rows_at = slice(head * keys, (head + 1) * keys)
            key_sum = jnp.where(col == head, key_full[rows_at], key_sum)
            value_sum = jnp.where(col == head, value_full[rows_at], value_sum)
        memory_ref[0, :, lanes] = key_sum * SCALE
        memory_ref[1, :, lanes] = value_sum

    each(rows, 64, first)
    back(crossed_ref, 2, keep)
    each(model, wide, cross)
    back(normed2_ref, 1, keep)
    each(rows, 64, second)
    back(attended_ref, 0, keep)
    if split:
        size = outs[0].shape[1]
        for out_ref, index in zip(outs, range(2)):
            out_ref[...] = work_ref[:, pl.ds(pl.multiple_of(place_ref[index] * size, size), size)].astype(BF)
    else:
        outs[0][...] = work_ref[...].astype(BF)


def middle_back(places, parts, at, cotangent, gu, more, kept, sources, plan, adapters, gains, keys, values):
    model = cotangent.shape[1]
    rows = kept[0].shape[0]
    spread = model // HEAD * keys.shape[0]
    flat = lambda dims: pl.BlockSpec(dims, lambda _, ref: (0,) * len(dims))
    block = pl.BlockSpec((rows, model), lambda _, ref: (at, 0))
    shapes = [jax.ShapeDtypeStruct((rows, model // parts), BF)] * parts + [
        jax.ShapeDtypeStruct((rows, model), F32),
        jax.ShapeDtypeStruct((2,) + keys.shape, F32),
        jax.ShapeDtypeStruct(adapters.shape, F32),
    ]
    return pl.pallas_call(
        partial(middle_back_kernel, plan, parts == 2),
        grid_spec=pltpu.PrefetchScalarGridSpec(
            num_scalar_prefetch=1,
            grid=(1,),
            in_specs=[pl.BlockSpec(memory_space=pl.ANY)] * len(sources)
            + [block, flat(gu.shape), flat(more.shape)]
            + [flat(item.shape) for item in kept]
            + [flat(item.shape) for item in (adapters, gains, keys, values)],
            out_specs=[flat(item.shape) for item in shapes],
            scratch_shapes=[
                pltpu.VMEM((3, model, model), BF),
                pltpu.VMEM((spread, 4 * HEAD), BF),
                pltpu.VMEM((spread, 4 * HEAD), BF),
                pltpu.VMEM((rows, model), F32),
                pltpu.VMEM((rows, model), BF),
                pltpu.SemaphoreType.DMA((3, 3)),
            ],
        ),
        out_shape=shapes,
        compiler_params=params(),
        cost_estimate=cost(6 * rows * model * model, 6 * model * model + 36 * rows * model),
        name="middle_back",
    )(places, *sources, cotangent, gu, more, *kept, adapters, gains, keys, values)


def qkv_grads_kernel(
    place_ref, grad_ref, normed_ref, lat_ref, up_ref, glat_ref, mine_ref, theirs_ref, glat_acc, gup_acc, down_acc,
    down_all, upper_all,
):
    at = pl.program_id(0)
    gradient = grad_ref[...]
    rank = mine_ref.shape[0]
    model = normed_ref.shape[1]
    width = gradient.shape[1]
    gup_acc[...] = mm_tn(lat_ref[...], gradient)

    @pl.when(at == 0)
    def _():
        glat_acc[...] = jnp.zeros_like(glat_acc)
        upper_all[...] = jnp.zeros_like(upper_all)

    into = pl.ds(pl.multiple_of(at * model + place_ref[0] * width, LANES), width)
    upper_all[:, into] = gup_acc[pl.ds(pl.multiple_of(at * rank, rank), rank), :].astype(BF)
    glat_acc[...] += mm_nt(gradient, up_ref[...])

    @pl.when(at == pl.num_programs(0) - 1)
    def _():
        low = glat_acc[...].astype(BF)
        glat_ref[...] = low
        down_acc[...] = mm_tn(low, normed_ref[...])
        for part in range(3):
            down_all[:, part * model : (part + 1) * model] = down_acc[part * rank : (part + 1) * rank, :].astype(BF)
        share(place_ref, down_all, upper_all, mine_ref, theirs_ref)


def share(place_ref, down_all, upper_all, mine_ref, theirs_ref):
    @pl.when(place_ref[0] == 0)
    def _():
        mine_ref[...] = down_all[...]
        theirs_ref[...] = upper_all[...]

    @pl.when(place_ref[0] != 0)
    def _():
        mine_ref[...] = upper_all[...]
        theirs_ref[...] = down_all[...]


def qkv_grads(places, gradient, normed, latent, up):
    frames, model = normed.shape
    parts, ranks, width = up.shape
    rank = ranks // parts
    table = jax.ShapeDtypeStruct((rank, parts * model), BF)
    return pl.pallas_call(
        qkv_grads_kernel,
        grid=(parts,),
        in_specs=[
            smem(),
            pl.BlockSpec((None, frames, width), lambda at: (at, 0, 0)),
            whole(normed.shape),
            whole(latent.shape),
            pl.BlockSpec((None, ranks, width), lambda at: (at, 0, 0)),
        ],
        out_specs=[whole(latent.shape), whole(table.shape), whole(table.shape)],
        out_shape=[jax.ShapeDtypeStruct(latent.shape, BF), table, table],
        scratch_shapes=[
            pltpu.VMEM(latent.shape, F32),
            pltpu.VMEM((ranks, width), F32),
            pltpu.VMEM((ranks, model), F32),
            pltpu.VMEM(table.shape, BF),
            pltpu.VMEM(table.shape, BF),
        ],
        compiler_params=params(1, 42 * MIB),
        cost_estimate=cost(8 * frames * ranks * width * parts, 2 * frames * (model + parts * width)),
        name="qkv_grads",
    )(places, gradient, normed, latent, up)


def qkv_back_kernel(place_ref, grad_ref, glat_ref, down_ref, w_ref, gu_ref, gu_acc):
    at = pl.program_id(0)
    model = gu_ref.shape[1]
    last = pl.num_programs(0) - 1

    def some(cols):
        direct = mm_nt(grad_ref[...], w_ref[cols, :])

        @pl.when(at == 0)
        def _():
            gu_acc[:, cols] = direct + mm(glat_ref[...], down_ref[:, cols])

        @pl.when(jnp.logical_and(at > 0, at < last))
        def _():
            gu_acc[:, cols] += direct

        @pl.when(at == last)
        def _():
            gu_ref[:, cols] = (gu_acc[:, cols] + direct).astype(gu_ref.dtype)

    each(model, 512, some)


def qkv_back(place, row_count, gradient, glat, down, packed, start, kind):
    ranks, model = down.shape
    width = gradient.shape[2]
    if start % width == 0 and width % LANES == 0:
        weight, spec = packed, pl.BlockSpec((model, width), lambda at, ref: (0, start // width + at))
    else:
        weight = packed[:, start : start + 3 * width].reshape(model, 3, width).transpose(1, 0, 2)
        spec = pl.BlockSpec((None, model, width), lambda at, ref: (at, 0, 0))
    return pl.pallas_call(
        qkv_back_kernel,
        grid_spec=pltpu.PrefetchScalarGridSpec(
            num_scalar_prefetch=1,
            grid=(3,),
            in_specs=[
                pl.BlockSpec((None, row_count, width), lambda at, ref: (at, ref[0], 0)),
                pl.BlockSpec((row_count, ranks), lambda at, ref: (ref[0], 0)),
                pl.BlockSpec(down.shape, lambda at, ref: (0, 0)),
                spec,
            ],
            out_specs=pl.BlockSpec((row_count, model), lambda at, ref: (0, 0)),
            scratch_shapes=[pltpu.VMEM((row_count, model), F32)],
        ),
        out_shape=jax.ShapeDtypeStruct((row_count, model), kind),
        compiler_params=params(1, 42 * MIB),
        cost_estimate=cost(6 * row_count * model * width, 6 * model * width + 8 * row_count * model),
        name="qkv_back",
    )(place, gradient, glat, down, weight)


def last_norm_kernel(blocks, frames_ref, ours_ref, theirs_ref, gain_ref, *refs):
    pieces, grad_ref = refs[:-1], refs[-1]
    at = pl.program_id(0)
    gradient = ours_ref[...] + theirs_ref[...].astype(F32)
    back = norm_back(frames_ref[...].astype(F32), gain_ref[...], gradient)
    for index, piece_ref in enumerate(pieces):

        @pl.when(at // blocks == index)
        def _(piece_ref=piece_ref):
            grad_ref[...] = back + piece_ref[...]


def last_norm(frames, ours, theirs, gains, pieces):
    rows, model = frames.shape
    step = min(128, rows)
    blocks = pieces[0].shape[0] // step
    block = pl.BlockSpec((step, model), lambda at: (at, 0))

    def piece_spec(index):
        return pl.BlockSpec((step, model), lambda at: (jnp.clip(at - index * blocks, 0, blocks - 1), 0))

    return pl.pallas_call(
        partial(last_norm_kernel, blocks),
        grid=(rows // step,),
        in_specs=[block, block, block, whole(gains.shape)] + [piece_spec(index) for index in range(len(pieces))],
        out_specs=block,
        out_shape=jax.ShapeDtypeStruct((rows, model), F32),
        compiler_params=params(1, 42 * MIB),
        cost_estimate=cost(20 * rows * model, 16 * rows * model),
        name="last_norm",
    )(frames, ours, theirs, gains, *pieces)


def run_length(size):
    count = 1
    while count * size % LANES:
        count *= 2
    return count


def join_kernel(pieces_ref, flat_ref):
    count, _, size = pieces_ref.shape
    run = run_length(size)

    def some(at, carry):
        parts = [pieces_ref[at * run + index] for index in range(run)]
        into = pl.ds(pl.multiple_of(at * run * size, LANES), run * size)
        flat_ref[:, into] = jnp.concatenate(parts, 1)
        return carry

    lax.fori_loop(0, count // run, some, 0)


def join_pieces(pieces):
    count, rows, size = pieces.shape
    if count % run_length(size):
        return pieces.transpose(1, 0, 2).reshape(rows, count * size)
    return pl.pallas_call(
        join_kernel,
        out_shape=jax.ShapeDtypeStruct((rows, count * size), pieces.dtype),
        compiler_params=params(0),
        name="join_pieces",
    )(pieces)


def split_kernel(*refs):
    sources, pieces_ref, flat_ref = refs[:-2], refs[-2], refs[-1]
    count, _, size = pieces_ref.shape
    run = run_length(size)
    start = 0
    for first_ref, second_ref in zip(sources[::2], sources[1::2]):
        width = first_ref.shape[1]
        both = first_ref[...].astype(F32) + second_ref[...].astype(F32)
        flat_ref[:, start : start + width] = both.astype(BF)
        start += width

    def some(at, carry):
        block = flat_ref[:, pl.ds(pl.multiple_of(at * run * size, LANES), run * size)]
        for index in range(run):
            pieces_ref[at * run + index] = block[:, index * size : (index + 1) * size]
        return carry

    lax.fori_loop(0, count // run, some, 0)


def split_sums(pairs, count):
    rows = pairs[0].shape[0]
    total = sum(item.shape[1] for item in pairs[::2])
    return pl.pallas_call(
        split_kernel,
        out_shape=jax.ShapeDtypeStruct((count, rows, total // count), BF),
        scratch_shapes=[pltpu.VMEM((rows, total), BF)],
        compiler_params=params(0, 42 * MIB),
        name="split_sums",
    )(*pairs)


def unit_loop(plan, work):
    fsdp, seq, folds, local = plan
    run = run_length(local)

    def some(at, carry):
        span = run * seq * folds * local
        block = pl.ds(pl.multiple_of(at * span, LANES), span)
        folded = [
            pl.ds(pl.multiple_of(fold * fsdp * local + at * run * local, LANES), run * local) for fold in range(folds)
        ]
        work(run, block, folded)
        return carry

    lax.fori_loop(0, fsdp // run, some, 0)


def take_units_kernel(plan, place_ref, all_ref, *refs):
    own_ref = refs[-1]
    _, seq, folds, local = plan
    spot = place_ref[0]

    def work(run, block, folded):
        values = all_ref[:, block]
        for fold, into in enumerate(folded):
            parts = []
            for index in range(run):
                base = (index * seq * folds + fold) * local
                part = values[:, base : base + local]
                for other in range(1, seq):
                    shift = base + other * folds * local
                    part = jnp.where(spot == other, values[:, shift : shift + local], part)
                parts.append(part)
            own_ref[:, into] = jnp.concatenate(parts, 1)

    unit_loop(plan, work)
    if len(refs) == 2:
        model = refs[0].shape[1]
        hidden = own_ref.shape[1] - folds * model
        for fold in range(folds):
            rows = pl.ds(pl.multiple_of((spot * folds + fold) * local, 16), local)
            own_ref[:, hidden + fold * model : hidden + (fold + 1) * model] = refs[0][rows, :]


def take_units(plan, places, matrix, low=None):
    _, seq, folds, local = plan
    rows, width = matrix.shape
    extra = [] if low is None else [low]
    out_width = width // seq + sum(folds * item.shape[1] for item in extra)
    return pl.pallas_call(
        partial(take_units_kernel, plan),
        in_specs=[smem()] + [pl.BlockSpec(memory_space=pltpu.VMEM)] * (1 + len(extra)),
        out_shape=jax.ShapeDtypeStruct((rows, out_width), matrix.dtype),
        compiler_params=params(0),
        name="take_units",
    )(places, matrix, *extra)


def collect_kernel(plan, blocks, place_ref, *refs):
    parts, squares, refs = refs[:blocks], refs[blocks : 2 * blocks], refs[2 * blocks :]
    feeds = [refs[at : at + 4] for at in range(0, len(refs) - 12, 4)]
    (
        other_ref, lat_ref, flat_ref, down_text_ref, text_ref, w_ref,
        mine_ref, theirs_ref, text_grad_ref, down_all, upper_all, unit_acc,
    ) = refs[-12:]
    _, seq, folds, local = plan
    rank = mine_ref.shape[0]
    model = text_ref.shape[1]
    wide = other_ref.shape[2]
    spot = place_ref[0]
    own = pl.ds(pl.multiple_of(spot * wide, wide), wide)

    def total(items, rows):
        value = items[0][rows, :]
        for item in items[1:]:
            value = value + item[rows, :]
        return value

    moved = []
    for part in range(2):
        value = parts[0][part, :, own]
        for item in parts[1:]:
            value = value + item[part, :, own]
        moved.append((value + other_ref[part].astype(F32)).astype(BF))
    moved = jnp.concatenate(moved, 1)
    glat = mm_nt(moved, flat_ref[...]).astype(BF)
    gup = mm_tn(lat_ref[...], moved)
    gdown = mm_tn(glat, text_ref[...])
    text_grad_ref[...] = (mm_nt(moved, w_ref[...]) + mm(glat, down_text_ref[...])).astype(BF)

    upper_all[:, 2 * model : 4 * model] = jnp.zeros((rank, 2 * model), BF)
    for part in range(2):
        rows = slice(part * rank, (part + 1) * rank)
        down_all[:, (2 + part) * model : (3 + part) * model] = gdown[rows].astype(BF)
        into = pl.ds(pl.multiple_of((2 + part) * model + spot * wide, LANES), wide)
        upper_all[:, into] = gup[rows, part * wide : (part + 1) * wide].astype(BF)
    for index, at in enumerate((0, 1, 4)):
        cols = slice(at * model, (at + 1) * model)
        down_all[:, cols] = total(squares, slice(2 * index * rank, (2 * index + 1) * rank)).astype(BF)
        upper_all[:, cols] = total(squares, slice((2 * index + 1) * rank, (2 * index + 2) * rank)).astype(BF)
    every = slice(0, rank)
    down_all[:, 5 * model : 6 * model] = total([item[0] for item in feeds], every).astype(BF)
    upper_all[:, upper_all.shape[1] - model :] = total([item[3] for item in feeds], every).astype(BF)
    for into_ref, start, which in ((upper_all, 5 * model, 1), (down_all, 6 * model, 2)):
        unit_acc[...] = total([item[which] for item in feeds], every)

        def work(run, block, folded):
            values = [unit_acc[:, cols] for cols in folded]
            spread = []
            for index in range(run):
                for other in range(seq):
                    for fold in range(folds):
                        part = values[fold][:, index * local : (index + 1) * local]
                        spread.append(jnp.where(spot == other, part, 0.0))
            at = pl.ds(pl.multiple_of(start + block.start, LANES), block.size)
            into_ref[:, at] = jnp.concatenate(spread, 1).astype(BF)

        unit_loop(plan, work)
    share(place_ref, down_all, upper_all, mine_ref, theirs_ref)


def collect(plan, places, parts, squares, feeds, other, lat_text, flat_text, down_text, text, packed, start):
    rank = squares[0].shape[0] // 6
    model = text.shape[1]
    hidden = feeds[0][1].shape[1]
    wide2 = flat_text.shape[1]
    width = 6 * model + hidden * plan[1]
    weight, spec = window(packed, start, wide2)
    feeds = [item for feed in feeds for item in feed]
    before = list(parts) + list(squares) + feeds + [other, lat_text, flat_text, down_text, text]
    table = jax.ShapeDtypeStruct((rank, width), BF)
    shapes = [table, table, jax.ShapeDtypeStruct(text.shape, BF)]
    return pl.pallas_call(
        partial(collect_kernel, plan, len(parts)),
        grid=(1,),
        in_specs=[smem()] + [whole(item.shape) for item in before] + [spec],
        out_specs=[whole(item.shape) for item in shapes],
        out_shape=shapes,
        scratch_shapes=[pltpu.VMEM(table.shape, BF)] * 2 + [pltpu.VMEM((rank, hidden), F32)],
        compiler_params=params(1),
        cost_estimate=cost(4 * text.shape[0] * model * wide2, 2 * model * wide2),
        name="collect",
    )(places, *before, weight)


def both_kernel(place_ref, mine_ref, other_ref, down_ref, upper_ref):
    first = place_ref[0] == 0
    for at in range(mine_ref.shape[0]):
        mine, other = mine_ref[at].astype(F32), other_ref[at].astype(F32)
        down_ref[at] = jnp.where(first, mine, other)
        upper_ref[at] = jnp.where(first, other, mine)


def both_tables(places, mine, other):
    return pl.pallas_call(
        both_kernel,
        in_specs=[smem()] + [pl.BlockSpec(memory_space=pltpu.VMEM)] * 2,
        out_shape=[jax.ShapeDtypeStruct(mine.shape, F32)] * 2,
        compiler_params=params(0, 42 * MIB),
        name="both_tables",
    )(places, mine, other)


def body(
    inputs,
    text_states,
    adapter_index,
    norm_gains,
    norm_biases,
    self_in,
    self_out,
    cross_query,
    cross_text,
    cross_out,
    hidden_in,
    hidden_out,
    adapter_down,
    adapter_up,
    cotangent,
    *,
    sizes,
):
    seq, fsdp = sizes
    spot = lax.axis_index("seq")
    first_here = spot == 0
    there = (seq - 1) - spot
    local = self_in.shape[0]
    depth = hidden_out.shape[0] // seq
    pair = seq == 2 and depth % local == 0 and fsdp % run_length(local) == 0
    model = inputs.shape[2]
    rows = inputs.shape[1]
    frames = rows * seq
    wide = model // seq
    hidden_all = hidden_in.shape[1]
    hidden = hidden_all // seq
    adapters, rank, piece = adapter_down.shape
    total = piece * fsdp

    blocks = max(rows // 256, 1)
    size = rows // blocks

    def swap(value):
        return lax.ppermute(value, "seq", [(0, 1), (1, 0)])

    def pick(value, axis, extent, which=None):
        return lax.dynamic_slice_in_dim(value, (spot if which is None else which) * extent, extent, axis)

    def ordered(mine, other):
        return jnp.where(first_here, mine, other), jnp.where(first_here, other, mine)

    def gather(value, axis):
        if pair:
            return jnp.concatenate(ordered(value, swap(value)), axis)
        return lax.all_gather(value, "seq", axis=axis, tiled=True)

    def after(value, *others):
        return lax.optimization_barrier((value,) + others)[0]

    def put(value, axis):
        shape = list(value.shape)
        shape[axis] = seq
        return lax.dynamic_update_slice_in_dim(jnp.zeros(shape, value.dtype), value, spot, axis)

    def own_columns(matrix, parts):
        return [pick(matrix[:, at * model : (at + 1) * model], 1, wide) for at in range(parts)]

    def flat_down(grads, parts):
        return jnp.concatenate([grads[at * rank : (at + 1) * rank] for at in range(parts)], 1)

    def flat_upper(own):
        return put(jnp.stack(own, 1)[:, :, None], 2).reshape(rank, len(own) * model)

    squares_here = [cross_out, cross_query] + [pick(self_out, 1, wide) if pair else self_out]
    first = squares_here + own_columns(self_in, 3) + own_columns(cross_text, 2)
    edges = [0]
    for item in first:
        edges.append(edges[-1] + item.shape[1])
    start_in, start_text = edges[3], edges[6]
    packed = lax.all_gather(jnp.concatenate(first, 1), "fsdp", axis=0, tiled=True)
    squares_plan = ((edges[2], None), (edges[1], None), (edges[0], None))
    if pair:
        squares_plan = ((edges[2], 1),) + squares_plan[1:]
    core = lax.rem(lax.axis_index("fsdp"), 2)
    where_here = jnp.stack([spot, there, core, 1 - core]).astype(jnp.int32)
    if pair:
        folds = depth // local
        plan = (fsdp, seq, folds, local)
        own_units = partial(take_units, plan, where_here)
        packed_feed = lax.all_gather(own_units(hidden_in, hidden_out), "fsdp", axis=0, tiled=True)

        def feed_weights(block):
            per = model // block
            return (
                packed_feed,
                pl.BlockSpec((model, block), lambda at: (0, at)),
                packed_feed,
                pl.BlockSpec((block, model), lambda at: (at % per, folds + at // per)),
            )
    else:

        def own_units(matrix):
            kept = lax.dynamic_index_in_dim(matrix.reshape(-1, fsdp, seq, depth), spot, 2, False)
            return kept.reshape(-1, hidden)

        def all_units(matrix):
            return put(matrix.reshape(-1, fsdp, 1, depth), 2).reshape(-1, hidden_all)

        whole_in = lax.all_gather(own_units(hidden_in), "fsdp", axis=0, tiled=True)
        whole_out = lax.all_gather(pick(hidden_out, 0, depth), "fsdp", axis=0, tiled=True)

        def feed_weights(block):
            return (
                whole_in,
                pl.BlockSpec((model, block), lambda at: (0, at)),
                whole_out,
                pl.BlockSpec((block, model), lambda at: (at, 0)),
            )

    index_all = lax.all_to_all(jnp.broadcast_to(adapter_index, (fsdp,)), "fsdp", 0, 0, tiled=True)
    if pair:
        table = jnp.where(first_here, adapter_down, adapter_up)
        mine = join_pieces(lax.all_to_all(jnp.take(table, index_all, axis=0), "fsdp", 0, 0, tiled=True))
        down_all, upper_all = ordered(mine, swap(mine))
    else:
        table = jnp.concatenate([adapter_down, adapter_up], 1)
        chosen = join_pieces(lax.all_to_all(jnp.take(table, index_all, axis=0), "fsdp", 0, 0, tiled=True))
        down_all, upper_all = chosen[:rank], chosen[rank:]
    in_cuts = [0, 3 * model, 4 * model, 5 * model, 7 * model, 8 * model, 9 * model, 9 * model + hidden_all]
    out_cuts = [0, 3 * model, 4 * model, 5 * model, 7 * model, 8 * model, 8 * model + hidden_all, 9 * model + hidden_all]
    downs = [down_all[:, in_cuts[at] : in_cuts[at + 1]] for at in range(7)]
    uppers = [upper_all[:, out_cuts[at] : out_cuts[at + 1]] for at in range(7)]

    def part_down(matrix, parts):
        return jnp.concatenate([matrix[:, at * model : (at + 1) * model] for at in range(parts)], 0)

    def part_upper(matrix, parts):
        own = own_columns(matrix, parts)
        return jnp.stack(
            [jnp.pad(item, ((at * rank, (parts - 1 - at) * rank), (0, 0))) for at, item in enumerate(own)], 0
        )

    units = own_units(jnp.concatenate([uppers[5], downs[6]], 0))
    feed_adapters = (downs[5], units[:rank], units[rank:], uppers[6])
    square_adapters = jnp.concatenate([downs[1], uppers[1], downs[2], uppers[2], downs[4], uppers[4]], 0)
    down_qkv, upper_qkv = part_down(downs[0], 3), part_upper(uppers[0], 3)
    down_text, upper_text = part_down(downs[3], 2), part_upper(uppers[3], 2)
    flat_text = jnp.concatenate([upper_text[0], upper_text[1]], 1)

    frames_in = inputs[0]
    cot = cotangent[0]
    if pair:
        frames_parts = [frames_in, swap(frames_in)]
        cot_other = swap(after(cot, frames_parts[1]))
    else:
        frames_parts = [lax.all_gather(frames_in, "seq", axis=0, tiled=True)]
    norm_places = where_here if pair else jnp.zeros((4,), jnp.int32)
    if pair:
        frames_parts[1] = after(frames_parts[1], cot_other, units)
    normed1, lat_qkv = norm_project(norm_places, frames_parts, norm_gains[0:1], norm_biases[0:1], down_qkv)
    packed = after(packed, normed1)
    sources = [packed]
    if pair:
        half = model // 2
        straight = swap(lax.dynamic_slice(packed, (core * half, edges[2]), (half, wide)))
    triple = qkv_project(normed1, lat_qkv, upper_qkv, packed, start_in, 3 * wide)
    padded = -(-wide // LANES) * LANES
    if padded != wide:
        triple = jnp.pad(triple.reshape(frames, 3, wide), ((0, 0), (0, 0), (0, padded - wide)))
        triple = triple.reshape(frames, 3 * padded)
    text = after(text_states[0], triple)
    w_text = packed[:, start_text : start_text + 2 * wide]
    lat_text = mm_nt(text, down_text).astype(BF)
    memory = (mm(text, w_text) + mm(lat_text, flat_text)).astype(BF)
    head_out, probs, *leaving = attend(where_here, [size] * blocks if pair else [], after(triple, memory), padded)

    if pair:
        neighbours = [(at, at ^ 1) for at in range(fsdp)]
        sources += [straight, lax.ppermute(after(straight, head_out), "fsdp", neighbours)]

    memory_all = gather(memory.reshape(-1, 2, wide), 2)
    keys, values = memory_all[:, 0], memory_all[:, 1]

    constants = (sources, squares_plan, square_adapters, norm_gains, norm_biases, keys, values)
    if pair:
        received = [swap(leaving[0])]
        for item in leaving[1:]:
            received.append(swap(after(item, received[-1])))
    else:
        natural = lax.all_to_all(head_out[:, :wide], "seq", split_axis=0, concat_axis=1, tiled=True)
    made = []
    for at in range(blocks):
        if pair:
            own, spec, others = head_out, (size, wide), [received[at]]
        else:
            own, spec, others = natural, (size, model), []
        ready = after(frames_in, made[-1][7]) if made else frames_in
        made.append(middle(where_here if pair else jnp.zeros((4,), jnp.int32), own, spec, others, ready, at, blocks, *constants))
    normed3 = [item[7] for item in made]
    resid2 = [item[6] for item in made]

    feed_tail = feed_adapters + (feed_weights, hidden)
    if pair:
        others = [swap(item) for item in normed3]
        ours = [feed_forward(normed3[:1], resid2[:1], cot, 0, *feed_tail, F32)]
        theirs = feed_forward([others[0], after(others[1], ours[0][0])] if blocks > 1 else others, [], cot_other, 0, *feed_tail, BF)
        out_leaving, gu_leaving = theirs[:blocks], theirs[blocks : 2 * blocks]
        gu_more = [swap(gu_leaving[0])]
        for at in range(1, blocks):
            ours.append(feed_forward([after(normed3[at], gu_leaving[0])], [resid2[at]], cot, at, *feed_tail, F32))
            gu_more.append(swap(after(gu_leaving[at], gu_more[-1], ours[-1][0])))
        gu = [item[1] for item in ours]
        out_more = []
        feed_grads = [item[2:] for item in ours] + [theirs[2 * blocks :]]
    else:
        wide_in = gather(jnp.concatenate(normed3, 0), 0)
        all_out = feed_forward([wide_in], [], gather(cot, 0), 0, *feed_tail, F32)
        summed = [
            lax.psum_scatter(item.astype(BF), "seq", scatter_dimension=0, tiled=True) for item in all_out[:2]
        ]
        output = (jnp.concatenate(resid2, 0) + summed[0].astype(F32)).astype(BF)
        gu = [summed[1][at * size : (at + 1) * size] for at in range(blocks)]
        gu_more = [jnp.zeros_like(item) for item in gu]
        feed_grads = [all_out[2:]]

    pieces, resid1_grads, memory_parts, square_parts = [], [], [], []
    for at in range(blocks):
        gu_here = gu[at] if at == 0 else after(gu[at], result[-3])
        kept = made[at][:7] + made[at][8:9]
        result = middle_back(
            where_here, 2 if pair else 1, at, cot, gu_here, gu_more[at],
            kept, sources, squares_plan, square_adapters, norm_gains, keys, values,
        )
        if pair:
            waited = [pieces[-1][1]] if at else []
            if at == 0:
                out_more.append(swap(after(out_leaving[0], result[0])))
            if at == blocks - 1:
                memory_part = sum(memory_parts, result[-2]).astype(BF)
                memory_other = swap(after(pick(memory_part, 2, wide, there), *out_more))
                waited.append(memory_other)
            pieces.append((result[0], swap(after(result[1], *waited) if waited else result[1])))
        else:
            pieces.append(result[0])
        resid1_grads.append(result[-3])
        memory_parts.append(result[-2])
        square_parts.append(result[-1])
    resid1_grad = jnp.concatenate(resid1_grads, 0)
    square_grads = sum(square_parts[1:], square_parts[0])

    if pair:
        early, early_leaving, text_low = collect(
            plan, where_here, memory_parts, square_parts, feed_grads, memory_other, lat_text, flat_text, down_text,
            text_states[0], packed, start_text,
        )
        grad_pieces = [item[0] for item in pieces] + [item[1] for item in pieces]
    else:
        head_grad = lax.all_to_all(jnp.concatenate(pieces, 0), "seq", split_axis=1, concat_axis=0, tiled=True)
        grad_pieces = [jnp.pad(head_grad, ((0, 0), (0, padded - wide)))]
    triple_grad = attend_back(where_here, triple, head_out, grad_pieces, probs, padded)[:, :, :wide]
    if pair:
        early_other = swap(after(early_leaving, pieces[-1][1]))
        for at in range(1, blocks):
            out_more.append(swap(after(out_leaving[at], early_other, triple_grad)))
        glat_qkv, late, late_leaving = qkv_grads(
            where_here, after(triple_grad, early_other), normed1, lat_qkv, upper_qkv
        )
        late_other = swap(late_leaving)
    else:
        glat_qkv = sum(mm_nt(triple_grad[at], upper_qkv[at]) for at in range(3)).astype(BF)
        gdown_qkv = mm_tn(glat_qkv, normed1)
        gup_qkv = [mm_tn(lat_qkv[:, at * rank : (at + 1) * rank], triple_grad[at]) for at in range(3)]
    back = partial(qkv_back, gradient=triple_grad, glat=glat_qkv, down=down_qkv, packed=packed, start=start_in)
    if pair:
        for_them = back(there[None], rows, kind=BF)
        for_us = back(after(spot, for_them, *out_more)[None], rows, kind=F32)
        input_grad = last_norm(frames_in, for_us, swap(for_them), norm_gains[0:1], resid1_grads)
        output = jnp.concatenate(
            [(item[0] + other.astype(F32)).astype(BF) for item, other in zip(ours, out_more)], 0
        )
    else:
        full = back(jnp.zeros((1,), jnp.int32), frames, kind=BF)
        normed1_grad = lax.psum_scatter(full, "seq", scatter_dimension=0, tiled=True).astype(F32)
        resid1_grad = jnp.concatenate(resid1_grads, 0)
        input_grad = resid1_grad + norm_back(frames_in.astype(F32), norm_gains[0:1], normed1_grad)

    selector = (index_all[None, :] == jnp.arange(adapters, dtype=jnp.int32)[:, None]).astype(BF)

    def by_adapter(sent, *others):
        received = lax.all_to_all(sent, "fsdp", 0, 0, tiled=True)
        chooser = after(selector, *others) if others else selector
        return jnp.einsum("ac,crw->arw", chooser, received, preferred_element_type=F32)

    if pair:
        shares = by_adapter(split_sums([after(late, for_them), late_other, early, early_other], fsdp), for_us).astype(BF)
        grad_down, grad_up = both_tables(where_here, shares, swap(shares))
        text_total = text_low.astype(F32) + swap(text_low).astype(F32)
    else:
        memory_part = sum(memory_parts[1:], memory_parts[0]).astype(BF)
        memory_grad = lax.psum_scatter(memory_part, "seq", scatter_dimension=2, tiled=True)
        memory_flat = jnp.concatenate([memory_grad[0], memory_grad[1]], 1)
        glat_text = mm_nt(memory_flat, flat_text).astype(BF)
        gup_text = mm_tn(lat_text, memory_flat)
        gdown_text = mm_tn(glat_text, text)
        text_low = (mm_nt(memory_flat, w_text) + mm(glat_text, down_text)).astype(BF)
        own_text = [gup_text[at * rank : (at + 1) * rank, at * wide : (at + 1) * wide] for at in range(2)]
        gdown_in, gup_in, gdown_out, gup_out = feed_grads[0]
        square_grads = sum(square_parts[1:], square_parts[0])
        squares = [square_grads[rank * at : rank * (at + 1)] for at in range(6)]
        down_sent = [flat_down(gdown_qkv, 3), squares[0], squares[2], flat_down(gdown_text, 2), squares[4], gdown_in]
        upper_sent = [flat_upper(gup_qkv), squares[1], squares[3], flat_upper(own_text), squares[5]]
        down_sent = jnp.concatenate(down_sent + [all_units(gdown_out)], 1)
        upper_sent = jnp.concatenate(upper_sent + [all_units(gup_in), gup_out], 1)
        sent = jnp.concatenate([down_sent, upper_sent], 0).astype(BF).reshape(2 * rank, fsdp, piece).transpose(1, 0, 2)
        shares = lax.psum(by_adapter(sent).astype(BF), "seq")
        grad_down, grad_up = shares[:, :rank], shares[:, rank:]
        text_total = lax.psum(text_low, "seq").astype(F32)
    return (output[None], input_grad[None], text_total[None], grad_down.astype(F32), grad_up.astype(F32))


def solution(mesh):
    return jax.shard_map(
        partial(body, sizes=(mesh.shape["seq"], mesh.shape["fsdp"])),
        mesh=mesh,
        in_specs=(
            P("fsdp", "seq", None),
            P("fsdp", None, None),
            P("fsdp"),
            P(),
            P(),
            P("fsdp", None),
            P("fsdp", None),
            P("fsdp", None),
            P("fsdp", None),
            P("fsdp", None),
            P("fsdp", None),
            P("fsdp", None),
            P(None, None, "fsdp"),
            P(None, None, "fsdp"),
            P("fsdp", "seq", None),
        ),
        out_specs=(
            P("fsdp", "seq", None),
            P("fsdp", "seq", None),
            P("fsdp", None, None),
            P(None, None, "fsdp"),
            P(None, None, "fsdp"),
        ),
        check_vma=False,
    )
```

profile of v0, /device:TPU:0, one launch (start us, length us, event | category | flops | bytes accessed | tf_op | source)
XLA Modules:
  0.0 493.2 jit_solution(4399186700788626187)
XLA Ops:
  18.8 7.4 %all-to-all-start = ((s32[16,1,1]{2,1,0:T(1,128)}), s32[16,1,1]{2,1,0:T(1,128)S(1)}, u32[]{:S(2)}, u32[]{:S(2)}) async-start(s32[16,1,1]{2,1,0:T(1,128)} %broadcast_in_dim.33), calls=%async_computation | async-start | bytes 16384 | tf_op jit(solution)/shard_map/all_to_all | solution.py:1170
  26.3 6.4 %all-to-all-done = s32[16,1,1]{2,1,0:T(1,128)S(1)} async-done(((s32[16,1,1]{2,1,0:T(1,128)}), s32[16,1,1]{2,1,0:T(1,128)S(1)}, u32[]{:S(2)}, u32[]{:S(2)}) %all-to-all-start) | async-done | bytes 96 | tf_op jit(solution)/shard_map/all_to_all | solution.py:1170
  40.6 25.7 %all-to-all-done.1.pieces_ref = bf16[16,16,1248]{2,1,0:T(8,128)(2,1)} async-done(((bf16[16,16,1248]{2,1,0:T(8,128)(2,1)}), bf16[16,16,1248]{2,1,0:T(8,128)(2,1)}, u32[]{:S(2)}, u32[]{:S(2)}) %all-to-all-start.1) | async-done | bytes 639008 | tf_op jit(solution)/shard_map/all_to_all | solution.py:1173
  77.9 12.2 %collective-permute-done.2 = bf16[16,19968]{1,0:T(8,128)(2,1)} collective-permute-done((bf16[16,19968]{1,0:T(8,128)(2,1)}, bf16[16,19968]{1,0:T(8,128)(2,1)}, u32[]{:S(2)}, u32[]{:S(2)}) %collective-permute-start.2) | collective-permute-done | bytes 639008 | tf_op jit(solution)/shard_map/ppermute | solution.py:1094
  96.9 26.2 %collective-permute-done.1.refs_2_ = bf16[512,1536]{1,0:T(8,128)(2,1)} collective-permute-done((bf16[512,1536]{1,0:T(8,128)(2,1)S(1)}, bf16[512,1536]{1,0:T(8,128)(2,1)}, u32[]{:S(2)}, u32[]{:S(2)}) %collective-permute-start.1) | collective-permute-done | bytes 1572896 | tf_op jit(solution)/shard_map/ppermute | solution.py:1094
  123.2 7.6 %norm_project.1 = (bf16[1024,1536]{1,0:T(8,128)(2,1)}, bf16[1024,48]{1,0:T(8,128)(2,1)}) custom-call(s32[4]{0:T(128)} %pad_add_fusion.place_ref, bf16[512,1536]{1,0:T(8,128)(2,1)} %bitcast.43, bf16[512,1536]{1,0:T(8,128)(2,1)} %collective-permute-done.refs_1_, f32[1,1536]{1,0:T(1,128)} %slice.118.refs_2_.gain_ref, f32[1,1536]{1,0:T(1,128)} %slice.119.refs_3_, ...), custom_call_target="tpu_custom_call" | custom-call | flops 150994944 | bytes 6291456 | tf_op jit(solution)/shard_map/norm_project/pallas_call | solution.py:113
  130.8 16.6 %all-gather.3.cloned.1.call-done.w_ref.refs_0_.refs_21_ = bf16[1536,7680]{1,0:T(8,128)(2,1)} async-done(((bf16[96,7680]{1,0:T(8,128)(2,1)}), bf16[1536,7680]{1,0:T(8,128)(2,1)}) %all-gather.3.cloned.1.call-update) | async-done | bytes 23592976 | tf_op jit(solution)/shard_map/all_gather | solution.py:1130
  152.2 12.4 %qkv_project.1.q_ref.k_ref.v_ref = bf16[1024,2304]{1,0:T(8,128)(2,1)S(1)} custom-call(bf16[1024,1536]{1,0:T(8,128)(2,1)S(1)} %copy-done.6, bf16[1024,48]{1,0:T(8,128)(2,1)S(1)} %copy-done.11, bf16[3,48,768]{2,1,0:T(8,128)(2,1)S(1)} %pad_maximum_fusion.1.up_ref, bf16[1536,7680]{1,0:T(8,128)(2,1)} %all-gather.3.cloned.1.call-done.w_ref.refs_0_.refs_21_), custom_call_target="tpu_custom_call" | custom-call | flops 7247757312 | bytes 10223616 | tf_op jit(solution)/shard_map/qkv_project/pallas_call | solution.py:147
  170.0 18.7 %attend.1 = (bf16[1024,768]{1,0:T(8,128)(2,1)}, bf16[12,2560,256]{2,1,0:T(8,128)(2,1)}, bf16[256,768]{1,0:T(8,128)(2,1)}, bf16[256,768]{1,0:T(8,128)(2,1)}) custom-call(s32[4]{0:T(128)} %pad_add_fusion.place_ref, bf16[1024,2304]{1,0:T(8,128)(2,1)} %copy-done, bf16[1024,2304]{1,0:T(8,128)(2,1)} %copy-done, bf16[1024,2304]{1,0:T(8,128)(2,1)} %copy-done), custom_call_target="tpu_custom_call" | custom-call | flops 2013265920 | bytes 22020096 | tf_op jit(solution)/shard_map/attend/pallas_call | solution.py:206
  196.7 7.9 %collective-permute-done.6.refs_10_ = bf16[256,768]{1,0:T(8,128)(2,1)S(1)} collective-permute-done((bf16[256,768]{1,0:T(8,128)(2,1)}, bf16[256,768]{1,0:T(8,128)(2,1)S(1)}, u32[]{:S(2)}, u32[]{:S(2)}) %collective-permute-start.6) | collective-permute-done | bytes 393248 | tf_op jit(solution)/shard_map/ppermute | solution.py:1094
  206.9 19.2 %middle.2 = (bf16[256,1536]{1,0:T(8,128)(2,1)}, f32[256,1536]{1,0:T(8,128)}, bf16[256,1536]{1,0:T(8,128)(2,1)}, bf16[256,1536]{1,0:T(8,128)(2,1)}, bf16[1536,256...) custom-call(s32[4]{0:T(128)} %pad_add_fusion.place_ref, ...), custom_call_target="tpu_custom_call" | custom-call | flops 3623878656 | bytes 23592960 | tf_op jit(solution)/shard_map/middle/pallas_call | solution.py:530
  228.6 19.2 %middle.3 = (bf16[256,1536]{1,0:T(8,128)(2,1)}, f32[256,1536]{1,0:T(8,128)}, bf16[256,1536]{1,0:T(8,128)(2,1)}, bf16[256,1536]{1,0:T(8,128)(2,1)}, bf16[1536,256...) custom-call(s32[4]{0:T(128)} %pad_add_fusion.place_ref, ...), custom_call_target="tpu_custom_call" | custom-call | flops 3623878656 | bytes 23592960 | tf_op jit(solution)/shard_map/middle/pallas_call | solution.py:530
  250.6 18.9 %feed_forward.3 = (f32[256,1536]{1,0:T(8,128)}, bf16[256,1536]{1,0:T(8,128)(2,1)}, f32[16,1536]{1,0:T(8,128)}, f32[16,3072]{1,0:T(8,128)}, f32[16,3072]{1,0:T(8,128)}, /*index=5*/f32[16,1536]{1,0:T(8,128)}) custom-call(bf16[256,1536]{1,0:T(8,128)(2,1)} %get-tuple-element.98.refs_0_, f32[256,1536]{1,0:T(8,128)} %get-tuple-element.99.refs_1_.refs_12_, ...), custom_call_target="tpu_custom_call" | custom-call | flops 9663676416 | bytes 18874368 | tf_op jit(solution)/shard_map/feed_forward/pallas_call | solution.py:368
  271.2 31.7 %feed_forward.4 = (bf16[256,1536]{1,0:T(8,128)(2,1)}, bf16[256,1536]{1,0:T(8,128)(2,1)}, bf16[256,1536]{1,0:T(8,128)(2,1)}, bf16[256,1536]{1,0:T(8,128)(2,1)}, f...) custom-call(bf16[256,1536]{1,0:T(8,128)(2,1)} %copy-done.50, ...), custom_call_target="tpu_custom_call" | custom-call | flops 19327352832 | bytes 18874368 | tf_op jit(solution)/shard_map/feed_forward/pallas_call | solution.py:368
  304.5 18.7 %feed_forward.5 = (f32[256,1536]{1,0:T(8,128)}, bf16[256,1536]{1,0:T(8,128)(2,1)}, f32[16,1536]{1,0:T(8,128)}, f32[16,3072]{1,0:T(8,128)}, f32[16,3072]{1,0:T(8,128)}, /*index=5*/f32[16,1536]{1,0:T(8,128)}) custom-call(bf16[256,1536]{1,0:T(8,128)(2,1)} %get-tuple-element.118.refs_0_, f32[256,1536]{1,0:T(8,128)} %get-tuple-element.119.refs_1_.refs_12_, ...), custom_call_target="tpu_custom_call" | custom-call | flops 9663676416 | bytes 18874368 | tf_op jit(solution)/shard_map/feed_forward/pallas_call | solution.py:368
  324.4 20.5 %middle_back.2 = (bf16[256,768]{1,0:T(8,128)(2,1)}, bf16[256,768]{1,0:T(8,128)(2,1)}, f32[256,1536]{1,0:T(8,128)}, f32[2,64,1536]{2,1,0:T(8,128)}, f32[96,1536]{1,0:T(8,128)}) custom-call(s32[4]{0:T(128)} %pad_add_fusion.place_ref, bf16[1536,7680]{1,0:T(8,128)(2,1)} %all-gather.3.cloned.1.call-done.w_ref.refs_0_.refs_21_, bf16[768,768]{1,0:T(8,128)(2,1)} %copy-done.20, ...), custom_call_target="tpu_custom_call" | custom-call | flops 3623878656 | bytes 28311552 | tf_op jit(solution)/shard_map/middle_back/pallas_call | solution.py:646
  347.9 20.5 %middle_back.3 = (bf16[256,768]{1,0:T(8,128)(2,1)}, bf16[256,768]{1,0:T(8,128)(2,1)}, f32[256,1536]{1,0:T(8,128)}, f32[2,64,1536]{2,1,0:T(8,128)}, f32[96,1536]{1,0:T(8,128)}) custom-call(s32[4]{0:T(128)} %pad_add_fusion.place_ref, bf16[1536,7680]{1,0:T(8,128)(2,1)} %all-gather.3.cloned.1.call-done.w_ref.refs_0_.refs_21_, bf16[768,768]{1,0:T(8,128)(2,1)} %copy-done.20, ...), custom_call_target="tpu_custom_call" | custom-call | flops 3623878656 | bytes 28311552 | tf_op jit(solution)/shard_map/middle_back/pallas_call | solution.py:646
  379.2 7.7 %collect.1 = (bf16[16,15360]{1,0:T(8,128)(2,1)}, bf16[16,15360]{1,0:T(8,128)(2,1)}, bf16[64,1536]{1,0:T(8,128)(2,1)}) custom-call(s32[4]{0:T(128)} %pad_add_fusion.place_ref, f32[2,64,1536]{2,1,0:T(8,128)} %get-tuple-element.122.refs_0_, f32[2,64,1536]{2,1,0:T(8,128)} %get-tuple-element.135.refs_1_, f32[96,1536]{1,0:T(8,128)} %get-tuple-element.136.refs_2_, ...), custom_call_target="tpu_custom_call" | custom-call | flops 603979776 | bytes 4718592 | tf_op jit(solution)/shard_map/collect/pallas_call | solution.py:1024
  389.6 20.8 %attend_back.1.grad_ref = bf16[3,1024,768]{2,1,0:T(8,128)(2,1)S(1)} custom-call(s32[4]{0:T(128)S(1)} %copy-done.15, bf16[1024,2304]{1,0:T(8,128)(2,1)} %copy-done, bf16[1024,2304]{1,0:T(8,128)(2,1)} %copy-done, bf16[1024,2304]{1,0:T(8,128)(2,1)} %copy-done, bf16[1024,768]{1,0:T(8,128)(2,1)S(1)} %copy-done.5, ...), custom_call_target="tpu_custom_call" | custom-call | flops 4026531840 | bytes 28311552 | tf_op jit(solution)/shard_map/attend_back/pallas_call | solution.py:275
  417.1 9.8 %qkv_back.2 = bf16[512,1536]{1,0:T(8,128)(2,1)} custom-call(s32[1]{0:T(128)} %bitcast.1.place_ref, bf16[3,1024,768]{2,1,0:T(8,128)(2,1)S(1)} %attend_back.1.grad_ref, bf16[1024,48]{1,0:T(8,128)(2,1)S(1)} %get-tuple-element.160.glat_ref, bf16[48,1536]{1,0:T(8,128)(2,1)S(1)} %copy-done.8, bf16[1536,7680]{1,0:T(8,128)(2,1)} %all-gather.3.cloned.1.call-done.w_ref.refs_0_.refs_21_), custom_call_target="tpu_custom_call" | custom-call | flops 3623878656 | bytes 13369344 | tf_op jit(solution)/shard_map/qkv_back/pallas_call | solution.py:775
  432.6 5.0 %all-to-all-start.2 = ((bf16[16,16,1248]{2,1,0:T(8,128)(2,1)}), bf16[16,16,1248]{2,1,0:T(8,128)(2,1)}, u32[]{:S(2)}, u32[]{:S(2)}) async-start(bf16[16,16,1248]{2,1,0:T(8,128)(2,1)} %split_sums.1), calls=%async_computation.2 | async-start | bytes 1310720 | tf_op jit(solution)/shard_map/all_to_all | solution.py:1340
  446.2 8.7 %qkv_back.3.ours_ref = f32[512,1536]{1,0:T(8,128)S(1)} custom-call(s32[1]{0:T(128)} %bitcast.15.place_ref, bf16[3,1024,768]{2,1,0:T(8,128)(2,1)S(1)} %copy-done.2, bf16[1024,48]{1,0:T(8,128)(2,1)S(1)} %get-tuple-element.160.glat_ref, bf16[48,1536]{1,0:T(8,128)(2,1)S(1)} %copy-done.8, bf16[1536,7680]{1,0:T(8,128)(2,1)} %all-gather.3.cloned.1.call-done.w_ref.refs_0_.refs_21_), custom_call_target="tpu_custom_call" | custom-call | flops 3623878656 | bytes 13369344 | tf_op jit(solution)/shard_map/qkv_back/pallas_call | solution.py:775
  460.3 17.4 %collective-permute-done.18.theirs_ref = bf16[512,1536]{1,0:T(8,128)(2,1)} collective-permute-done((bf16[512,1536]{1,0:T(8,128)(2,1)}, bf16[512,1536]{1,0:T(8,128)(2,1)}, u32[]{:S(2)}, u32[]{:S(2)}) %collective-permute-start.18) | collective-permute-done | bytes 1572896 | tf_op jit(solution)/shard_map/ppermute | solution.py:1094
  478.5 5.1 %last_norm.1 = f32[512,1536]{1,0:T(8,128)} custom-call(bf16[512,1536]{1,0:T(8,128)(2,1)S(1)} %bitcast.47, f32[512,1536]{1,0:T(8,128)S(1)} %qkv_back.3.ours_ref, bf16[512,1536]{1,0:T(8,128)(2,1)} %collective-permute-done.18.theirs_ref, f32[1,1536]{1,0:T(1,128)S(1)} %copy-done.18, f32[256,1536]{1,0:T(8,128)S(1)} %copy-done.9, f32[256,1536]{1,0:T(8,128)S(1)} %copy-done.10), custom_call_target="tpu_custom_call" | custom-call | flops 15728640 | bytes 12582912 | tf_op jit(solution)/shard_map/last_norm/pallas_call | solution.py:817
  (214 shorter events, 113.1 us)
Async XLA Ops:
  7.2 140.3 %all-gather.3.cloned.1.call-start = ((), (), s32[]{:S(2)}) async-start(), calls=%async_computation.3 | async-start | bytes 25067520 | tf_op jit(solution)/shard_map/all_gather | solution.py:1130
  12.7 237.9 %all-gather.5.cloned.1.call-start = ((), (), s32[]{:S(2)}) async-start(), calls=%async_computation.4 | async-start | bytes 20054016 | tf_op jit(solution)/shard_map/all_gather | solution.py:1140
  18.8 13.8 %all-to-all-start = ((s32[16,1,1]{2,1,0:T(1,128)}), s32[16,1,1]{2,1,0:T(1,128)S(1)}, u32[]{:S(2)}, u32[]{:S(2)}) async-start(s32[16,1,1]{2,1,0:T(1,128)} %broadcast_in_dim.33), calls=%async_computation | async-start | bytes 16384 | tf_op jit(solution)/shard_map/all_to_all | solution.py:1170
  34.6 31.6 %all-to-all-start.1 = ((bf16[16,16,1248]{2,1,0:T(8,128)(2,1)}), bf16[16,16,1248]{2,1,0:T(8,128)(2,1)}, u32[]{:S(2)}, u32[]{:S(2)}) async-start(bf16[16,16,1248]{2,1,0:T(8,128)(2,1)} %broadcast_select_fusion), calls=%async_computation.1 | async-start | bytes 1310720 | tf_op jit(solution)/shard_map/all_to_all | solution.py:1173
  39.1 37.4 %collective-permute-start = (bf16[512,1536]{1,0:T(8,128)(2,1)S(1)}, bf16[512,1536]{1,0:T(8,128)(2,1)}, u32[]{:S(2)}, u32[]{:S(2)}) collective-permute-start(bf16[512,1536]{1,0:T(8,128)(2,1)S(1)} %bitcast.46), channel_id=1, source_target_pairs={{0,16},{16,0},{1,17},{17,1},{2,18},{18,2},{3,19},{19,3},{4,20},{20... | collective-permute-start | bytes 4718600 | tf_op jit(solution)/shard_map/ppermute | solution.py:1094
  68.6 21.5 %collective-permute-start.2 = (bf16[16,19968]{1,0:T(8,128)(2,1)}, bf16[16,19968]{1,0:T(8,128)(2,1)}, u32[]{:S(2)}, u32[]{:S(2)}) collective-permute-start(bf16[16,19968]{1,0:T(8,128)(2,1)} %join_pieces.1), channel_id=1, source_target_pairs={{0,16},{16,0},{1,17},{17,1},{2,18},{18,2},{3,19},{19,3},{4,20},{20... | collective-permute-start | bytes 1916936 | tf_op jit(solution)/shard_map/ppermute | solution.py:1094
  76.5 46.7 %collective-permute-start.1 = (bf16[512,1536]{1,0:T(8,128)(2,1)S(1)}, bf16[512,1536]{1,0:T(8,128)(2,1)}, u32[]{:S(2)}, u32[]{:S(2)}) collective-permute-start(bf16[512,1536]{1,0:T(8,128)(2,1)S(1)} %bitcast.52), channel_id=1, source_target_pairs={{0,16},{16,0},{1,17},{17,1},{2,18},{18,2},{3,19},{19,3},{4,20},{20... | collective-permute-start | bytes 4718600 | tf_op jit(solution)/shard_map/ppermute | solution.py:1094
  148.8 39.9 %collective-permute-start.3 = (bf16[768,768]{1,0:T(8,128)(2,1)S(1)}, bf16[768,768]{1,0:T(8,128)(2,1)S(1)}, u32[]{:S(2)}, u32[]{:S(2)}) collective-permute-start(bf16[768,768]{1,0:T(8,128)(2,1)S(1)} %constant_dynamic-slice_fusion.5), channel_id=1, source_target_pairs={{0,16},{16,0},{1,17},{17,1},{2,18},{18,2},{3,19},{19,3},{4,20},{20... | collective-permute-start | bytes 3538952 | tf_op jit(solution)/shard_map/ppermute | solution.py:1094
  188.7 17.1 %collective-permute-start.4 = (bf16[768,768]{1,0:T(8,128)(2,1)S(1)}, bf16[768,768]{1,0:T(8,128)(2,1)S(1)}, u32[]{:S(2)}, u32[]{:S(2)}) collective-permute-start(bf16[768,768]{1,0:T(8,128)(2,1)S(1)} %collective-permute-done.3.refs_1_), channel_id=1, source_target_pairs={{0,1},{1,0},{2,3},{3,2},{4,5},{5,4},{6,7},{7,6},{8,9},{9,8},{10,11... | collective-permute-start | bytes 3538952 | tf_op jit(solution)/shard_map/ppermute | solution.py:1229
  189.4 15.2 %collective-permute-start.6 = (bf16[256,768]{1,0:T(8,128)(2,1)}, bf16[256,768]{1,0:T(8,128)(2,1)S(1)}, u32[]{:S(2)}, u32[]{:S(2)}) collective-permute-start(bf16[256,768]{1,0:T(8,128)(2,1)} %get-tuple-element.97), channel_id=1, source_target_pairs={{0,16},{16,0},{1,17},{17,1},{2,18},{18,2},{3,19},{19,3},{4,20},{20... | collective-permute-start | bytes 1179656 | tf_op jit(solution)/shard_map/ppermute | solution.py:1094
  204.6 23.3 %collective-permute-start.8 = (bf16[256,768]{1,0:T(8,128)(2,1)}, bf16[256,768]{1,0:T(8,128)(2,1)S(1)}, u32[]{:S(2)}, u32[]{:S(2)}) collective-permute-start(bf16[256,768]{1,0:T(8,128)(2,1)} %get-tuple-element.103), channel_id=1, source_target_pairs={{0,16},{16,0},{1,17},{17,1},{2,18},{18,2},{3,19},{19,3},{4,20},{20... | collective-permute-start | bytes 1179656 | tf_op jit(solution)/shard_map/ppermute | solution.py:1094
  226.1 43.4 %collective-permute-start.7 = (bf16[256,1536]{1,0:T(8,128)(2,1)}, bf16[256,1536]{1,0:T(8,128)(2,1)S(1)}, u32[]{:S(2)}, u32[]{:S(2)}) collective-permute-start(bf16[256,1536]{1,0:T(8,128)(2,1)} %get-tuple-element.98.refs_0_), channel_id=1, source_target_pairs={{0,16},{16,0},{1,17},{17,1},{2,18},{18,2},{3,19},{19,3},{4,20},{20... | collective-permute-start | bytes 2359304 | tf_op jit(solution)/shard_map/ppermute | solution.py:1094
  247.9 21.6 %collective-permute-start.9 = (bf16[256,1536]{1,0:T(8,128)(2,1)}, bf16[256,1536]{1,0:T(8,128)(2,1)S(1)}, u32[]{:S(2)}, u32[]{:S(2)}) collective-permute-start(bf16[256,1536]{1,0:T(8,128)(2,1)} %get-tuple-element.118.refs_0_), channel_id=1, source_target_pairs={{0,16},{16,0},{1,17},{17,1},{2,18},{18,2},{3,19},{19,3},{4,20},{20... | collective-permute-start | bytes 2359304 | tf_op jit(solution)/shard_map/ppermute | solution.py:1094
  302.9 20.2 %collective-permute-start.10 = (bf16[256,1536]{1,0:T(8,128)(2,1)}, bf16[256,1536]{1,0:T(8,128)(2,1)S(1)}, u32[]{:S(2)}, u32[]{:S(2)}) collective-permute-start(bf16[256,1536]{1,0:T(8,128)(2,1)} %get-tuple-element.108), channel_id=1, source_target_pairs={{0,16},{16,0},{1,17},{17,1},{2,18},{18,2},{3,19},{19,3},{4,20},{20... | collective-permute-start | bytes 2359304 | tf_op jit(solution)/shard_map/ppermute | solution.py:1094
  323.2 23.8 %collective-permute-start.12 = (bf16[256,1536]{1,0:T(8,128)(2,1)}, bf16[256,1536]{1,0:T(8,128)(2,1)S(1)}, u32[]{:S(2)}, u32[]{:S(2)}) collective-permute-start(bf16[256,1536]{1,0:T(8,128)(2,1)} %get-tuple-element.127), channel_id=1, source_target_pairs={{0,16},{16,0},{1,17},{17,1},{2,18},{18,2},{3,19},{19,3},{4,20},{20... | collective-permute-start | bytes 2359304 | tf_op jit(solution)/shard_map/ppermute | solution.py:1094
  344.9 24.5 %collective-permute-start.11 = (bf16[256,1536]{1,0:T(8,128)(2,1)}, bf16[256,1536]{1,0:T(8,128)(2,1)S(1)}, u32[]{:S(2)}, u32[]{:S(2)}) collective-permute-start(bf16[256,1536]{1,0:T(8,128)(2,1)} %get-tuple-element.117), channel_id=1, source_target_pairs={{0,16},{16,0},{1,17},{17,1},{2,18},{18,2},{3,19},{19,3},{4,20},{20... | collective-permute-start | bytes 2359304 | tf_op jit(solution)/shard_map/ppermute | solution.py:1094
  345.8 28.2 %collective-permute-start.14 = (bf16[256,768]{1,0:T(8,128)(2,1)}, bf16[256,768]{1,0:T(8,128)(2,1)S(1)}, u32[]{:S(2)}, u32[]{:S(2)}) collective-permute-start(bf16[256,768]{1,0:T(8,128)(2,1)} %get-tuple-element.153), channel_id=1, source_target_pairs={{0,16},{16,0},{1,17},{17,1},{2,18},{18,2},{3,19},{19,3},{4,20},{20... | collective-permute-start | bytes 1179656 | tf_op jit(solution)/shard_map/ppermute | solution.py:1094
  386.9 23.5 %collective-permute-start.16 = (bf16[16,15360]{1,0:T(8,128)(2,1)}, bf16[16,15360]{1,0:T(8,128)(2,1)S(1)}, u32[]{:S(2)}, u32[]{:S(2)}) collective-permute-start(bf16[16,15360]{1,0:T(8,128)(2,1)} %get-tuple-element.155), channel_id=1, source_target_pairs={{0,16},{16,0},{1,17},{17,1},{2,18},{18,2},{3,19},{19,3},{4,20},{20... | collective-permute-start | bytes 1474568 | tf_op jit(solution)/shard_map/ppermute | solution.py:1094
  388.6 52.7 %collective-permute-start.19 = (bf16[64,1536]{1,0:T(8,128)(2,1)}, bf16[64,1536]{1,0:T(8,128)(2,1)}, u32[]{:S(2)}, u32[]{:S(2)}) collective-permute-start(bf16[64,1536]{1,0:T(8,128)(2,1)} %get-tuple-element.163), channel_id=1, source_target_pairs={{0,16},{16,0},{1,17},{17,1},{2,18},{18,2},{3,19},{19,3},{4,20},{20... | collective-permute-start | bytes 589832 | tf_op jit(solution)/shard_map/ppermute | solution.py:1094
  410.4 32.7 %collective-permute-start.17 = (bf16[256,1536]{1,0:T(8,128)(2,1)}, bf16[256,1536]{1,0:T(8,128)(2,1)S(1)}, u32[]{:S(2)}, u32[]{:S(2)}) collective-permute-start(bf16[256,1536]{1,0:T(8,128)(2,1)} %get-tuple-element.158), channel_id=1, source_target_pairs={{0,16},{16,0},{1,17},{17,1},{2,18},{18,2},{3,19},{19,3},{4,20},{20... | collective-permute-start | bytes 2359304 | tf_op jit(solution)/shard_map/ppermute | solution.py:1094
  416.1 15.1 %collective-permute-start.20 = (bf16[16,4608]{1,0:T(8,128)(2,1)S(1)}, bf16[16,4608]{1,0:T(8,128)(2,1)S(1)}, u32[]{:S(2)}, u32[]{:S(2)}) collective-permute-start(bf16[16,4608]{1,0:T(8,128)(2,1)S(1)} %get-tuple-element.167), channel_id=1, source_target_pairs={{0,16},{16,0},{1,17},{17,1},{2,18},{18,2},{3,19},{19,3},{4,20},{20... | collective-permute-start | bytes 442376 | tf_op jit(solution)/shard_map/ppermute | solution.py:1094
  432.6 22.3 %all-to-all-start.2 = ((bf16[16,16,1248]{2,1,0:T(8,128)(2,1)}), bf16[16,16,1248]{2,1,0:T(8,128)(2,1)}, u32[]{:S(2)}, u32[]{:S(2)}) async-start(bf16[16,16,1248]{2,1,0:T(8,128)(2,1)} %split_sums.1), calls=%async_computation.2 | async-start | bytes 1310720 | tf_op jit(solution)/shard_map/all_to_all | solution.py:1340
  440.2 37.5 %collective-permute-start.18 = (bf16[512,1536]{1,0:T(8,128)(2,1)}, bf16[512,1536]{1,0:T(8,128)(2,1)}, u32[]{:S(2)}, u32[]{:S(2)}) collective-permute-start(bf16[512,1536]{1,0:T(8,128)(2,1)} %qkv_back.2), channel_id=1, source_target_pairs={{0,16},{16,0},{1,17},{17,1},{2,18},{18,2},{3,19},{19,3},{4,20},{20... | collective-permute-start | bytes 4718600 | tf_op jit(solution)/shard_map/ppermute | solution.py:1094
  456.5 27.7 %collective-permute-start.21 = (bf16[8,16,1248]{2,1,0:T(8,128)(2,1)S(1)}, bf16[8,16,1248]{2,1,0:T(8,128)(2,1)S(1)}, u32[]{:S(2)}, u32[]{:S(2)}) collective-permute-start(bf16[8,16,1248]{2,1,0:T(8,128)(2,1)S(1)} %copy.51.mine_ref), channel_id=1, source_target_pairs={{0,16},{16,0},{1,17},{17,1},{2,18},{18,2},{3,19},{19,3},{4,20},{20... | collective-permute-start | bytes 958472 | tf_op jit(solution)/shard_map/ppermute | solution.py:1094
  (55 other events, 865.1 us)
Sparse Core Ops, SparseCore 0:
  12.8 134.5 all-gather.2
  149.0 101.5 all-gather.4
where the time goes:
time: 503 us; the launch traced here: 493 us
  Pallas kernels  256 us (51%)
  waiting for transfers between devices  135 us (27%)
  starting transfers between devices  40.8 us (8%)
  local copies, waits for them, and re-layouts  23.1 us (5%)
  between operations  15.9 us (3%)
  other arithmetic  15.6 us (3%)
  matrix products  6.77 us (1%)
    ppermute x21, waiting for transfers between devices, swap(): return lax.ppermute(value, 'seq', [(0, 1), (1, 0)])  84.1 us
    pallas_call x3, Pallas kernels, feed_forward(): pl.pallas_call(partial(feed_kernel, len(pieces), len(bases)), grid=(hidde...  69.2 us
    pallas_call x2, Pallas kernels, middle_back(): pl.pallas_call(partial(middle_back_kernel, plan, parts == 2), grid_spec=p...  41 us
    pallas_call x2, Pallas kernels, middle(): pl.pallas_call(partial(middle_kernel, plan), grid_spec=pltpu.PrefetchScal...  38.5 us
    all_to_all x1, waiting for transfers between devices, body(): lax.all_to_all(jnp.take(table, index_all, axis=0), 'fsdp', 0, 0, tiled=True)  25.7 us
    ppermute x21, starting transfers between devices, swap(): return lax.ppermute(value, 'seq', [(0, 1), (1, 0)])  23.8 us
    pallas_call x1, Pallas kernels, attend_back(): pl.pallas_call(attend_back_kernel, grid=(pairs,), in_specs=[smem()] + pai...  20.8 us
    pallas_call x1, Pallas kernels, attend(): pl.pallas_call(attend_kernel, grid=(pairs,), in_specs=[smem()] + pair_spe...  18.7 us
  transfers between devices with their start and end apart: 27, of which 14 were waited for; matrix products, arithmetic and copies ran while one was open for 6% of the time, Pallas kernels for 45%

commit v1 on v0

--- a/solution.py
+++ b/solution.py
@@ -793,11 +793,10 @@
     )(place, gradient, glat, down, weight)
 
 
-def last_norm_kernel(blocks, frames_ref, ours_ref, theirs_ref, gain_ref, *refs):
+def last_norm_kernel(blocks, frames_ref, gradient_ref, gain_ref, *refs):
     pieces, grad_ref = refs[:-1], refs[-1]
     at = pl.program_id(0)
-    gradient = ours_ref[...] + theirs_ref[...].astype(F32)
-    back = norm_back(frames_ref[...].astype(F32), gain_ref[...], gradient)
+    back = norm_back(frames_ref[...].astype(F32), gain_ref[...], gradient_ref[...])
     for index, piece_ref in enumerate(pieces):
 
         @pl.when(at // blocks == index)
@@ -805,7 +804,7 @@
             grad_ref[...] = back + piece_ref[...]
 
 
-def last_norm(frames, ours, theirs, gains, pieces):
+def last_norm(frames, gradient, gains, pieces):
     rows, model = frames.shape
     step = min(128, rows)
     blocks = pieces[0].shape[0] // step
@@ -817,13 +816,13 @@
     return pl.pallas_call(
         partial(last_norm_kernel, blocks),
         grid=(rows // step,),
-        in_specs=[block, block, block, whole(gains.shape)] + [piece_spec(index) for index in range(len(pieces))],
+        in_specs=[block, block, whole(gains.shape)] + [piece_spec(index) for index in range(len(pieces))],
         out_specs=block,
         out_shape=jax.ShapeDtypeStruct((rows, model), F32),
         compiler_params=params(1, 42 * MIB),
         cost_estimate=cost(20 * rows * model, 16 * rows * model),
         name="last_norm",
-    )(frames, ours, theirs, gains, *pieces)
+    )(frames, gradient, gains, *pieces)
 
 
 def run_length(size):
@@ -1324,7 +1323,7 @@
     if pair:
         for_them = back(there[None], rows, kind=BF)
         for_us = back(after(spot, for_them, *out_more)[None], rows, kind=F32)
-        input_grad = last_norm(frames_in, for_us, swap(for_them), norm_gains[0:1], resid1_grads)
+        input_grad = last_norm(frames_in, for_us + swap(for_them).astype(F32), norm_gains[0:1], resid1_grads)
         output = jnp.concatenate(
             [(item[0] + other.astype(F32)).astype(BF) for item, other in zip(ours, out_more)], 0
         )
@@ -1342,8 +1341,8 @@
         return jnp.einsum("ac,crw->arw", chooser, received, preferred_element_type=F32)
 
     if pair:
-        shares = by_adapter(split_sums([after(late, for_them), late_other, early, early_other], fsdp), for_us).astype(BF)
-        grad_down, grad_up = both_tables(where_here, shares, swap(shares))
+        shares = by_adapter(split_sums([after(late, for_them), late_other, early, early_other], fsdp)).astype(BF)
+        grad_down, grad_up = both_tables(where_here, shares, swap(after(shares, for_us)))
         text_total = text_low.astype(F32) + swap(text_low).astype(F32)
     else:
         memory_part = sum(memory_parts[1:], memory_parts[0]).astype(BF)

time: 503 us -> 493 us (0.980)
    ppermute x21, waiting for transfers between devices: 84.1 us -> 75.9 us  [swap(): return lax.ppermute(value, 'seq', [(0, 1), (1, 0)])]
    unnamed x115 -> x95, local copies, waits for them, and re-layouts: 14.6 us -> 9.91 us
  transfers between devices with their start and end apart: 27 -> 27, of which waited for: 14 -> 15; matrix products, arithmetic and copies ran while one was open for 6% -> 6% of each run, Pallas kernels for 45% -> 46%
where the time goes in v1:
time: 493 us; the launch traced here: 483 us
  Pallas kernels  255 us (52%)
  waiting for transfers between devices  130 us (26%)
  starting transfers between devices  41 us (8%)
  local copies, waits for them, and re-layouts  18.5 us (4%)
  other arithmetic  16.1 us (3%)
  between operations  15.9 us (3%)
  matrix products  6.65 us (1%)
    ppermute x21, waiting for transfers between devices, swap(): return lax.ppermute(value, 'seq', [(0, 1), (1, 0)])  75.9 us
    pallas_call x3, Pallas kernels, feed_forward(): pl.pallas_call(partial(feed_kernel, len(pieces), len(bases)), grid=(hidde...  69.3 us
    pallas_call x2, Pallas kernels, middle_back(): pl.pallas_call(partial(middle_back_kernel, plan, parts == 2), grid_spec=p...  40.9 us
    pallas_call x2, Pallas kernels, middle(): pl.pallas_call(partial(middle_kernel, plan), grid_spec=pltpu.PrefetchScal...  38.6 us
    all_to_all x1, waiting for transfers between devices, body(): lax.all_to_all(jnp.take(table, index_all, axis=0), 'fsdp', 0, 0, tiled=True)  25.7 us
    ppermute x21, starting transfers between devices, swap(): return lax.ppermute(value, 'seq', [(0, 1), (1, 0)])  24 us
    pallas_call x1, Pallas kernels, attend_back(): pl.pallas_call(attend_back_kernel, grid=(pairs,), in_specs=[smem()] + pai...  20.8 us
    pallas_call x1, Pallas kernels, attend(): pl.pallas_call(attend_kernel, grid=(pairs,), in_specs=[smem()] + pair_spe...  18.7 us
  transfers between devices with their start and end apart: 27, of which 15 were waited for; matrix products, arithmetic and copies ran while one was open for 6% of the time, Pallas kernels for 46%

profile of v1, /device:TPU:0, one launch (start us, length us, event | category | flops | bytes accessed | tf_op | source)
XLA Modules:
  0.0 483.3 jit_solution(4008284733196202002)
XLA Ops:
  18.9 7.4 %all-to-all-start = ((s32[16,1,1]{2,1,0:T(1,128)}), s32[16,1,1]{2,1,0:T(1,128)S(1)}, u32[]{:S(2)}, u32[]{:S(2)}) async-start(s32[16,1,1]{2,1,0:T(1,128)} %broadcast_in_dim.33), calls=%async_computation | async-start | bytes 16384 | tf_op jit(solution)/shard_map/all_to_all | solution.py:1169
  26.3 6.4 %all-to-all-done = s32[16,1,1]{2,1,0:T(1,128)S(1)} async-done(((s32[16,1,1]{2,1,0:T(1,128)}), s32[16,1,1]{2,1,0:T(1,128)S(1)}, u32[]{:S(2)}, u32[]{:S(2)}) %all-to-all-start) | async-done | bytes 96 | tf_op jit(solution)/shard_map/all_to_all | solution.py:1169
  40.7 25.7 %all-to-all-done.1.pieces_ref = bf16[16,16,1248]{2,1,0:T(8,128)(2,1)} async-done(((bf16[16,16,1248]{2,1,0:T(8,128)(2,1)}), bf16[16,16,1248]{2,1,0:T(8,128)(2,1)}, u32[]{:S(2)}, u32[]{:S(2)}) %all-to-all-start.1) | async-done | bytes 639008 | tf_op jit(solution)/shard_map/all_to_all | solution.py:1172
  78.1 12.2 %collective-permute-done.2 = bf16[16,19968]{1,0:T(8,128)(2,1)} collective-permute-done((bf16[16,19968]{1,0:T(8,128)(2,1)}, bf16[16,19968]{1,0:T(8,128)(2,1)}, u32[]{:S(2)}, u32[]{:S(2)}) %collective-permute-start.2) | collective-permute-done | bytes 639008 | tf_op jit(solution)/shard_map/ppermute | solution.py:1093
  97.0 26.3 %collective-permute-done.1.refs_2_ = bf16[512,1536]{1,0:T(8,128)(2,1)} collective-permute-done((bf16[512,1536]{1,0:T(8,128)(2,1)S(1)}, bf16[512,1536]{1,0:T(8,128)(2,1)}, u32[]{:S(2)}, u32[]{:S(2)}) %collective-permute-start.1) | collective-permute-done | bytes 1572896 | tf_op jit(solution)/shard_map/ppermute | solution.py:1093
  123.2 7.6 %norm_project.1 = (bf16[1024,1536]{1,0:T(8,128)(2,1)}, bf16[1024,48]{1,0:T(8,128)(2,1)}) custom-call(s32[4]{0:T(128)} %pad_add_fusion.place_ref, bf16[512,1536]{1,0:T(8,128)(2,1)} %bitcast.43, bf16[512,1536]{1,0:T(8,128)(2,1)} %collective-permute-done.refs_1_, f32[1,1536]{1,0:T(1,128)} %slice.118.refs_2_.gain_ref, f32[1,1536]{1,0:T(1,128)} %slice.119.refs_3_, ...), custom_call_target="tpu_custom_call" | custom-call | flops 150994944 | bytes 6291456 | tf_op jit(solution)/shard_map/norm_project/pallas_call | solution.py:113
  130.9 16.5 %all-gather.3.cloned.1.call-done.w_ref.refs_0_.refs_21_ = bf16[1536,7680]{1,0:T(8,128)(2,1)} async-done(((bf16[96,7680]{1,0:T(8,128)(2,1)}), bf16[1536,7680]{1,0:T(8,128)(2,1)}) %all-gather.3.cloned.1.call-update) | async-done | bytes 23592976 | tf_op jit(solution)/shard_map/all_gather | solution.py:1129
  152.2 12.4 %qkv_project.1.q_ref.k_ref.v_ref = bf16[1024,2304]{1,0:T(8,128)(2,1)S(1)} custom-call(bf16[1024,1536]{1,0:T(8,128)(2,1)S(1)} %copy-done.6, bf16[1024,48]{1,0:T(8,128)(2,1)S(1)} %copy-done.11, bf16[3,48,768]{2,1,0:T(8,128)(2,1)S(1)} %pad_maximum_fusion.1.up_ref, bf16[1536,7680]{1,0:T(8,128)(2,1)} %all-gather.3.cloned.1.call-done.w_ref.refs_0_.refs_21_), custom_call_target="tpu_custom_call" | custom-call | flops 7247757312 | bytes 10223616 | tf_op jit(solution)/shard_map/qkv_project/pallas_call | solution.py:147
  170.0 18.7 %attend.1 = (bf16[1024,768]{1,0:T(8,128)(2,1)}, bf16[12,2560,256]{2,1,0:T(8,128)(2,1)}, bf16[256,768]{1,0:T(8,128)(2,1)}, bf16[256,768]{1,0:T(8,128)(2,1)}) custom-call(s32[4]{0:T(128)} %pad_add_fusion.place_ref, bf16[1024,2304]{1,0:T(8,128)(2,1)} %copy-done, bf16[1024,2304]{1,0:T(8,128)(2,1)} %copy-done, bf16[1024,2304]{1,0:T(8,128)(2,1)} %copy-done), custom_call_target="tpu_custom_call" | custom-call | flops 2013265920 | bytes 22020096 | tf_op jit(solution)/shard_map/attend/pallas_call | solution.py:206
  196.7 7.9 %collective-permute-done.6.refs_10_ = bf16[256,768]{1,0:T(8,128)(2,1)S(1)} collective-permute-done((bf16[256,768]{1,0:T(8,128)(2,1)}, bf16[256,768]{1,0:T(8,128)(2,1)S(1)}, u32[]{:S(2)}, u32[]{:S(2)}) %collective-permute-start.6) | collective-permute-done | bytes 393248 | tf_op jit(solution)/shard_map/ppermute | solution.py:1093
  206.9 19.2 %middle.2 = (bf16[256,1536]{1,0:T(8,128)(2,1)}, f32[256,1536]{1,0:T(8,128)}, bf16[256,1536]{1,0:T(8,128)(2,1)}, bf16[256,1536]{1,0:T(8,128)(2,1)}, bf16[1536,256...) custom-call(s32[4]{0:T(128)} %pad_add_fusion.place_ref, ...), custom_call_target="tpu_custom_call" | custom-call | flops 3623878656 | bytes 23592960 | tf_op jit(solution)/shard_map/middle/pallas_call | solution.py:530
  227.9 19.4 %middle.3 = (bf16[256,1536]{1,0:T(8,128)(2,1)}, f32[256,1536]{1,0:T(8,128)}, bf16[256,1536]{1,0:T(8,128)(2,1)}, bf16[256,1536]{1,0:T(8,128)(2,1)}, bf16[1536,256...) custom-call(s32[4]{0:T(128)} %pad_add_fusion.place_ref, ...), custom_call_target="tpu_custom_call" | custom-call | flops 3623878656 | bytes 23592960 | tf_op jit(solution)/shard_map/middle/pallas_call | solution.py:530
  250.6 18.9 %feed_forward.3 = (f32[256,1536]{1,0:T(8,128)}, bf16[256,1536]{1,0:T(8,128)(2,1)}, f32[16,1536]{1,0:T(8,128)}, f32[16,3072]{1,0:T(8,128)}, f32[16,3072]{1,0:T(8,128)}, /*index=5*/f32[16,1536]{1,0:T(8,128)}) custom-call(bf16[256,1536]{1,0:T(8,128)(2,1)} %get-tuple-element.98.refs_0_, f32[256,1536]{1,0:T(8,128)} %get-tuple-element.99.refs_1_.refs_12_, ...), custom_call_target="tpu_custom_call" | custom-call | flops 9663676416 | bytes 18874368 | tf_op jit(solution)/shard_map/feed_forward/pallas_call | solution.py:368
  271.3 31.7 %feed_forward.4 = (bf16[256,1536]{1,0:T(8,128)(2,1)}, bf16[256,1536]{1,0:T(8,128)(2,1)}, bf16[256,1536]{1,0:T(8,128)(2,1)}, bf16[256,1536]{1,0:T(8,128)(2,1)}, f...) custom-call(bf16[256,1536]{1,0:T(8,128)(2,1)} %copy-done.40, ...), custom_call_target="tpu_custom_call" | custom-call | flops 19327352832 | bytes 18874368 | tf_op jit(solution)/shard_map/feed_forward/pallas_call | solution.py:368
  304.5 18.7 %feed_forward.5 = (f32[256,1536]{1,0:T(8,128)}, bf16[256,1536]{1,0:T(8,128)(2,1)}, f32[16,1536]{1,0:T(8,128)}, f32[16,3072]{1,0:T(8,128)}, f32[16,3072]{1,0:T(8,128)}, /*index=5*/f32[16,1536]{1,0:T(8,128)}) custom-call(bf16[256,1536]{1,0:T(8,128)(2,1)} %get-tuple-element.118.refs_0_, f32[256,1536]{1,0:T(8,128)} %get-tuple-element.119.refs_1_.refs_12_, ...), custom_call_target="tpu_custom_call" | custom-call | flops 9663676416 | bytes 18874368 | tf_op jit(solution)/shard_map/feed_forward/pallas_call | solution.py:368
  324.5 20.5 %middle_back.2 = (bf16[256,768]{1,0:T(8,128)(2,1)}, bf16[256,768]{1,0:T(8,128)(2,1)}, f32[256,1536]{1,0:T(8,128)}, f32[2,64,1536]{2,1,0:T(8,128)}, f32[96,1536]{1,0:T(8,128)}) custom-call(s32[4]{0:T(128)} %pad_add_fusion.place_ref, bf16[1536,7680]{1,0:T(8,128)(2,1)} %all-gather.3.cloned.1.call-done.w_ref.refs_0_.refs_21_, bf16[768,768]{1,0:T(8,128)(2,1)} %copy-done.19, ...), custom_call_target="tpu_custom_call" | custom-call | flops 3623878656 | bytes 28311552 | tf_op jit(solution)/shard_map/middle_back/pallas_call | solution.py:646
  348.0 20.5 %middle_back.3 = (bf16[256,768]{1,0:T(8,128)(2,1)}, bf16[256,768]{1,0:T(8,128)(2,1)}, f32[256,1536]{1,0:T(8,128)}, f32[2,64,1536]{2,1,0:T(8,128)}, f32[96,1536]{1,0:T(8,128)}) custom-call(s32[4]{0:T(128)} %pad_add_fusion.place_ref, bf16[1536,7680]{1,0:T(8,128)(2,1)} %all-gather.3.cloned.1.call-done.w_ref.refs_0_.refs_21_, bf16[768,768]{1,0:T(8,128)(2,1)} %copy-done.19, ...), custom_call_target="tpu_custom_call" | custom-call | flops 3623878656 | bytes 28311552 | tf_op jit(solution)/shard_map/middle_back/pallas_call | solution.py:646
  379.2 7.7 %collect.1 = (bf16[16,15360]{1,0:T(8,128)(2,1)}, bf16[16,15360]{1,0:T(8,128)(2,1)}, bf16[64,1536]{1,0:T(8,128)(2,1)}) custom-call(s32[4]{0:T(128)} %pad_add_fusion.place_ref, f32[2,64,1536]{2,1,0:T(8,128)} %get-tuple-element.122.refs_0_, f32[2,64,1536]{2,1,0:T(8,128)} %get-tuple-element.135.refs_1_, f32[96,1536]{1,0:T(8,128)} %get-tuple-element.136.refs_2_, ...), custom_call_target="tpu_custom_call" | custom-call | flops 603979776 | bytes 4718592 | tf_op jit(solution)/shard_map/collect/pallas_call | solution.py:1023
  390.5 20.8 %attend_back.1.grad_ref = bf16[3,1024,768]{2,1,0:T(8,128)(2,1)S(1)} custom-call(s32[4]{0:T(128)S(1)} %copy-done.15, bf16[1024,2304]{1,0:T(8,128)(2,1)} %copy-done, bf16[1024,2304]{1,0:T(8,128)(2,1)} %copy-done, bf16[1024,2304]{1,0:T(8,128)(2,1)} %copy-done, bf16[1024,768]{1,0:T(8,128)(2,1)S(1)} %copy-done.5, ...), custom_call_target="tpu_custom_call" | custom-call | flops 4026531840 | bytes 28311552 | tf_op jit(solution)/shard_map/attend_back/pallas_call | solution.py:275
  418.1 9.8 %qkv_back.2 = bf16[512,1536]{1,0:T(8,128)(2,1)} custom-call(s32[1]{0:T(128)} %bitcast.1.place_ref, bf16[3,1024,768]{2,1,0:T(8,128)(2,1)S(1)} %attend_back.1.grad_ref, bf16[1024,48]{1,0:T(8,128)(2,1)S(1)} %get-tuple-element.160.glat_ref, bf16[48,1536]{1,0:T(8,128)(2,1)S(1)} %copy-done.8, bf16[1536,7680]{1,0:T(8,128)(2,1)} %all-gather.3.cloned.1.call-done.w_ref.refs_0_.refs_21_), custom_call_target="tpu_custom_call" | custom-call | flops 3623878656 | bytes 13369344 | tf_op jit(solution)/shard_map/qkv_back/pallas_call | solution.py:775
  428.9 6.1 %collective-permute-done.20.refs_1_ = bf16[16,4608]{1,0:T(8,128)(2,1)S(1)} collective-permute-done((bf16[16,4608]{1,0:T(8,128)(2,1)S(1)}, bf16[16,4608]{1,0:T(8,128)(2,1)S(1)}, u32[]{:S(2)}, u32[]{:S(2)}) %collective-permute-start.20) | collective-permute-done | bytes 147488 | tf_op jit(solution)/shard_map/ppermute | solution.py:1093
  436.4 5.0 %all-to-all-start.2 = ((bf16[16,16,1248]{2,1,0:T(8,128)(2,1)}), bf16[16,16,1248]{2,1,0:T(8,128)(2,1)}, u32[]{:S(2)}, u32[]{:S(2)}) async-start(bf16[16,16,1248]{2,1,0:T(8,128)(2,1)} %split_sums.1), calls=%async_computation.2 | async-start | bytes 1310720 | tf_op jit(solution)/shard_map/all_to_all | solution.py:1339
  446.4 8.7 %qkv_back.3 = f32[512,1536]{1,0:T(8,128)S(1)} custom-call(s32[1]{0:T(128)} %bitcast.15.place_ref, bf16[3,1024,768]{2,1,0:T(8,128)(2,1)S(1)} %copy-done.2, bf16[1024,48]{1,0:T(8,128)(2,1)S(1)} %get-tuple-element.160.glat_ref, bf16[48,1536]{1,0:T(8,128)(2,1)S(1)} %copy-done.8, bf16[1536,7680]{1,0:T(8,128)(2,1)} %all-gather.3.cloned.1.call-done.w_ref.refs_0_.refs_21_), custom_call_target="tpu_custom_call" | custom-call | flops 3623878656 | bytes 13369344 | tf_op jit(solution)/shard_map/qkv_back/pallas_call | solution.py:775
  460.7 8.1 %collective-permute-done.18 = bf16[512,1536]{1,0:T(8,128)(2,1)} collective-permute-done((bf16[512,1536]{1,0:T(8,128)(2,1)}, bf16[512,1536]{1,0:T(8,128)(2,1)}, u32[]{:S(2)}, u32[]{:S(2)}) %collective-permute-start.18) | collective-permute-done | bytes 1572896 | tf_op jit(solution)/shard_map/ppermute | solution.py:1093
  (194 shorter events, 111.3 us)
Async XLA Ops:
  7.2 140.3 %all-gather.3.cloned.1.call-start = ((), (), s32[]{:S(2)}) async-start(), calls=%async_computation.3 | async-start | bytes 25067520 | tf_op jit(solution)/shard_map/all_gather | solution.py:1129
  12.7 237.9 %all-gather.5.cloned.1.call-start = ((), (), s32[]{:S(2)}) async-start(), calls=%async_computation.4 | async-start | bytes 20054016 | tf_op jit(solution)/shard_map/all_gather | solution.py:1139
  18.9 13.8 %all-to-all-start = ((s32[16,1,1]{2,1,0:T(1,128)}), s32[16,1,1]{2,1,0:T(1,128)S(1)}, u32[]{:S(2)}, u32[]{:S(2)}) async-start(s32[16,1,1]{2,1,0:T(1,128)} %broadcast_in_dim.33), calls=%async_computation | async-start | bytes 16384 | tf_op jit(solution)/shard_map/all_to_all | solution.py:1169
  34.7 31.6 %all-to-all-start.1 = ((bf16[16,16,1248]{2,1,0:T(8,128)(2,1)}), bf16[16,16,1248]{2,1,0:T(8,128)(2,1)}, u32[]{:S(2)}, u32[]{:S(2)}) async-start(bf16[16,16,1248]{2,1,0:T(8,128)(2,1)} %broadcast_select_fusion), calls=%async_computation.1 | async-start | bytes 1310720 | tf_op jit(solution)/shard_map/all_to_all | solution.py:1172
  39.1 37.4 %collective-permute-start = (bf16[512,1536]{1,0:T(8,128)(2,1)S(1)}, bf16[512,1536]{1,0:T(8,128)(2,1)}, u32[]{:S(2)}, u32[]{:S(2)}) collective-permute-start(bf16[512,1536]{1,0:T(8,128)(2,1)S(1)} %bitcast.46), channel_id=1, source_target_pairs={{0,16},{16,0},{1,17},{17,1},{2,18},{18,2},{3,19},{19,3},{4,20},{20... | collective-permute-start | bytes 4718600 | tf_op jit(solution)/shard_map/ppermute | solution.py:1093
  68.7 21.5 %collective-permute-start.2 = (bf16[16,19968]{1,0:T(8,128)(2,1)}, bf16[16,19968]{1,0:T(8,128)(2,1)}, u32[]{:S(2)}, u32[]{:S(2)}) collective-permute-start(bf16[16,19968]{1,0:T(8,128)(2,1)} %join_pieces.1), channel_id=1, source_target_pairs={{0,16},{16,0},{1,17},{17,1},{2,18},{18,2},{3,19},{19,3},{4,20},{20... | collective-permute-start | bytes 1916936 | tf_op jit(solution)/shard_map/ppermute | solution.py:1093
  76.5 46.7 %collective-permute-start.1 = (bf16[512,1536]{1,0:T(8,128)(2,1)S(1)}, bf16[512,1536]{1,0:T(8,128)(2,1)}, u32[]{:S(2)}, u32[]{:S(2)}) collective-permute-start(bf16[512,1536]{1,0:T(8,128)(2,1)S(1)} %bitcast.52), channel_id=1, source_target_pairs={{0,16},{16,0},{1,17},{17,1},{2,18},{18,2},{3,19},{19,3},{4,20},{20... | collective-permute-start | bytes 4718600 | tf_op jit(solution)/shard_map/ppermute | solution.py:1093
  148.8 39.9 %collective-permute-start.3 = (bf16[768,768]{1,0:T(8,128)(2,1)S(1)}, bf16[768,768]{1,0:T(8,128)(2,1)S(1)}, u32[]{:S(2)}, u32[]{:S(2)}) collective-permute-start(bf16[768,768]{1,0:T(8,128)(2,1)S(1)} %constant_dynamic-slice_fusion.5), channel_id=1, source_target_pairs={{0,16},{16,0},{1,17},{17,1},{2,18},{18,2},{3,19},{19,3},{4,20},{20... | collective-permute-start | bytes 3538952 | tf_op jit(solution)/shard_map/ppermute | solution.py:1093
  188.7 17.1 %collective-permute-start.4 = (bf16[768,768]{1,0:T(8,128)(2,1)S(1)}, bf16[768,768]{1,0:T(8,128)(2,1)S(1)}, u32[]{:S(2)}, u32[]{:S(2)}) collective-permute-start(bf16[768,768]{1,0:T(8,128)(2,1)S(1)} %collective-permute-done.3.refs_1_), channel_id=1, source_target_pairs={{0,1},{1,0},{2,3},{3,2},{4,5},{5,4},{6,7},{7,6},{8,9},{9,8},{10,11... | collective-permute-start | bytes 3538952 | tf_op jit(solution)/shard_map/ppermute | solution.py:1228
  189.4 15.2 %collective-permute-start.6 = (bf16[256,768]{1,0:T(8,128)(2,1)}, bf16[256,768]{1,0:T(8,128)(2,1)S(1)}, u32[]{:S(2)}, u32[]{:S(2)}) collective-permute-start(bf16[256,768]{1,0:T(8,128)(2,1)} %get-tuple-element.97), channel_id=1, source_target_pairs={{0,16},{16,0},{1,17},{17,1},{2,18},{18,2},{3,19},{19,3},{4,20},{20... | collective-permute-start | bytes 1179656 | tf_op jit(solution)/shard_map/ppermute | solution.py:1093
  204.6 23.3 %collective-permute-start.8 = (bf16[256,768]{1,0:T(8,128)(2,1)}, bf16[256,768]{1,0:T(8,128)(2,1)}, u32[]{:S(2)}, u32[]{:S(2)}) collective-permute-start(bf16[256,768]{1,0:T(8,128)(2,1)} %get-tuple-element.103), channel_id=1, source_target_pairs={{0,16},{16,0},{1,17},{17,1},{2,18},{18,2},{3,19},{19,3},{4,20},{20... | collective-permute-start | bytes 1179656 | tf_op jit(solution)/shard_map/ppermute | solution.py:1093
  226.1 43.4 %collective-permute-start.7 = (bf16[256,1536]{1,0:T(8,128)(2,1)}, bf16[256,1536]{1,0:T(8,128)(2,1)S(1)}, u32[]{:S(2)}, u32[]{:S(2)}) collective-permute-start(bf16[256,1536]{1,0:T(8,128)(2,1)} %get-tuple-element.98.refs_0_), channel_id=1, source_target_pairs={{0,16},{16,0},{1,17},{17,1},{2,18},{18,2},{3,19},{19,3},{4,20},{20... | collective-permute-start | bytes 2359304 | tf_op jit(solution)/shard_map/ppermute | solution.py:1093
  247.2 22.3 %collective-permute-start.9 = (bf16[256,1536]{1,0:T(8,128)(2,1)}, bf16[256,1536]{1,0:T(8,128)(2,1)S(1)}, u32[]{:S(2)}, u32[]{:S(2)}) collective-permute-start(bf16[256,1536]{1,0:T(8,128)(2,1)} %get-tuple-element.118.refs_0_), channel_id=1, source_target_pairs={{0,16},{16,0},{1,17},{17,1},{2,18},{18,2},{3,19},{19,3},{4,20},{20... | collective-permute-start | bytes 2359304 | tf_op jit(solution)/shard_map/ppermute | solution.py:1093
  303.0 20.2 %collective-permute-start.10 = (bf16[256,1536]{1,0:T(8,128)(2,1)}, bf16[256,1536]{1,0:T(8,128)(2,1)S(1)}, u32[]{:S(2)}, u32[]{:S(2)}) collective-permute-start(bf16[256,1536]{1,0:T(8,128)(2,1)} %get-tuple-element.108), channel_id=1, source_target_pairs={{0,16},{16,0},{1,17},{17,1},{2,18},{18,2},{3,19},{19,3},{4,20},{20... | collective-permute-start | bytes 2359304 | tf_op jit(solution)/shard_map/ppermute | solution.py:1093
  323.3 23.8 %collective-permute-start.12 = (bf16[256,1536]{1,0:T(8,128)(2,1)}, bf16[256,1536]{1,0:T(8,128)(2,1)S(1)}, u32[]{:S(2)}, u32[]{:S(2)}) collective-permute-start(bf16[256,1536]{1,0:T(8,128)(2,1)} %get-tuple-element.127), channel_id=1, source_target_pairs={{0,16},{16,0},{1,17},{17,1},{2,18},{18,2},{3,19},{19,3},{4,20},{20... | collective-permute-start | bytes 2359304 | tf_op jit(solution)/shard_map/ppermute | solution.py:1093
  345.0 24.5 %collective-permute-start.11 = (bf16[256,1536]{1,0:T(8,128)(2,1)}, bf16[256,1536]{1,0:T(8,128)(2,1)S(1)}, u32[]{:S(2)}, u32[]{:S(2)}) collective-permute-start(bf16[256,1536]{1,0:T(8,128)(2,1)} %get-tuple-element.117), channel_id=1, source_target_pairs={{0,16},{16,0},{1,17},{17,1},{2,18},{18,2},{3,19},{19,3},{4,20},{20... | collective-permute-start | bytes 2359304 | tf_op jit(solution)/shard_map/ppermute | solution.py:1093
  345.9 28.2 %collective-permute-start.14 = (bf16[256,768]{1,0:T(8,128)(2,1)}, bf16[256,768]{1,0:T(8,128)(2,1)S(1)}, u32[]{:S(2)}, u32[]{:S(2)}) collective-permute-start(bf16[256,768]{1,0:T(8,128)(2,1)} %get-tuple-element.153), channel_id=1, source_target_pairs={{0,16},{16,0},{1,17},{17,1},{2,18},{18,2},{3,19},{19,3},{4,20},{20... | collective-permute-start | bytes 1179656 | tf_op jit(solution)/shard_map/ppermute | solution.py:1093
  387.0 24.3 %collective-permute-start.16 = (bf16[16,15360]{1,0:T(8,128)(2,1)}, bf16[16,15360]{1,0:T(8,128)(2,1)S(1)}, u32[]{:S(2)}, u32[]{:S(2)}) collective-permute-start(bf16[16,15360]{1,0:T(8,128)(2,1)} %get-tuple-element.155), channel_id=1, source_target_pairs={{0,16},{16,0},{1,17},{17,1},{2,18},{18,2},{3,19},{19,3},{4,20},{20... | collective-permute-start | bytes 1474568 | tf_op jit(solution)/shard_map/ppermute | solution.py:1093
  389.4 52.0 %collective-permute-start.19 = (bf16[64,1536]{1,0:T(8,128)(2,1)}, bf16[64,1536]{1,0:T(8,128)(2,1)S(1)}, u32[]{:S(2)}, u32[]{:S(2)}) collective-permute-start(bf16[64,1536]{1,0:T(8,128)(2,1)} %get-tuple-element.163), channel_id=1, source_target_pairs={{0,16},{16,0},{1,17},{17,1},{2,18},{18,2},{3,19},{19,3},{4,20},{20... | collective-permute-start | bytes 589832 | tf_op jit(solution)/shard_map/ppermute | solution.py:1093
  411.3 31.9 %collective-permute-start.17 = (bf16[256,1536]{1,0:T(8,128)(2,1)S(1)}, bf16[256,1536]{1,0:T(8,128)(2,1)}, u32[]{:S(2)}, u32[]{:S(2)}) collective-permute-start(bf16[256,1536]{1,0:T(8,128)(2,1)S(1)} %copy-done.39), channel_id=1, source_target_pairs={{0,16},{16,0},{1,17},{17,1},{2,18},{18,2},{3,19},{19,3},{4,20},{20... | collective-permute-start | bytes 2359304 | tf_op jit(solution)/shard_map/ppermute | solution.py:1093
  417.0 18.0 %collective-permute-start.20 = (bf16[16,4608]{1,0:T(8,128)(2,1)S(1)}, bf16[16,4608]{1,0:T(8,128)(2,1)S(1)}, u32[]{:S(2)}, u32[]{:S(2)}) collective-permute-start(bf16[16,4608]{1,0:T(8,128)(2,1)S(1)} %get-tuple-element.166), channel_id=1, source_target_pairs={{0,16},{16,0},{1,17},{17,1},{2,18},{18,2},{3,19},{19,3},{4,20},{20... | collective-permute-start | bytes 442376 | tf_op jit(solution)/shard_map/ppermute | solution.py:1093
  427.9 41.0 %collective-permute-start.18 = (bf16[512,1536]{1,0:T(8,128)(2,1)}, bf16[512,1536]{1,0:T(8,128)(2,1)}, u32[]{:S(2)}, u32[]{:S(2)}) collective-permute-start(bf16[512,1536]{1,0:T(8,128)(2,1)} %qkv_back.2), channel_id=1, source_target_pairs={{0,16},{16,0},{1,17},{17,1},{2,18},{18,2},{3,19},{19,3},{4,20},{20... | collective-permute-start | bytes 4718600 | tf_op jit(solution)/shard_map/ppermute | solution.py:1093
  436.4 21.7 %all-to-all-start.2 = ((bf16[16,16,1248]{2,1,0:T(8,128)(2,1)}), bf16[16,16,1248]{2,1,0:T(8,128)(2,1)}, u32[]{:S(2)}, u32[]{:S(2)}) async-start(bf16[16,16,1248]{2,1,0:T(8,128)(2,1)} %split_sums.1), calls=%async_computation.2 | async-start | bytes 1310720 | tf_op jit(solution)/shard_map/all_to_all | solution.py:1339
  459.6 14.7 %collective-permute-start.21 = (bf16[8,16,1248]{2,1,0:T(8,128)(2,1)S(1)}, bf16[8,16,1248]{2,1,0:T(8,128)(2,1)S(1)}, u32[]{:S(2)}, u32[]{:S(2)}) collective-permute-start(bf16[8,16,1248]{2,1,0:T(8,128)(2,1)S(1)} %copy.51.mine_ref), channel_id=1, source_target_pairs={{0,16},{16,0},{1,17},{17,1},{2,18},{18,2},{3,19},{19,3},{4,20},{20... | collective-permute-start | bytes 958472 | tf_op jit(solution)/shard_map/ppermute | solution.py:1093
  (45 other events, 448.0 us)
Sparse Core Ops, SparseCore 0:
  12.8 134.5 all-gather.2
  149.0 101.5 all-gather.4
